TPU v7x, 512 devices: a whole 4x8x8 slice. The times are simulated.
512 devices in a mesh: ka: 16 (over y, core), op: 4 (over x), row: 8 (over z).
Axes of the slice: x: 4, y: 8, z: 8, core: 2. Of those that a mesh axis runs over, the one named last changes fastest.
Arguments:
- kgrid: int32 [3, 4096], P(None, ('ka', 'op', 'row')), may hold values from 0 to 63
- rvec: int32 [3, 256], replicated, may hold values from -8 to 8
- degen: int32 [256], replicated, may hold values from 1 to 4
- operators: bfloat16 [4, 256, 12800], P('op', ('ka', 'row')), may hold values from -1 to 1
- vectors: bfloat16 [4096, 12800], P(('ka', 'op', 'row')), may hold values from -0.5 to 0.5
Outputs:
- density: float32 [3, 4096], P(None, ('ka', 'op', 'row'))
- magnetization: float32 [3], replicated
All inputs are finite; a program needn't handle non-finite values.
Results may differ from a plain program's by a relative error of at most 0.012.
Values may be sent and summed in bfloat16 or wider, within the bound.
A program may use at most 64 MiB of HBM per device.

v0:
```python
import functools
import math

import jax
import jax.numpy as jnp
from jax import lax
from jax.sharding import Mesh
from jax.sharding import PartitionSpec as P

W = 80
GRID = 64
KA = ("ka_0", "ka_1")
KA_ROW = ("ka_0", "ka_1", "row")
KA_OP_ROW = ("ka_0", "ka_1", "op", "row")


SMEARING = 0.5


def sent_to_all(shard, axis):
    count = lax.axis_size(axis)
    return lax.all_to_all(
        jnp.broadcast_to(shard[None], (count, *shard.shape)), axis, 0, 0, tiled=True
    )


def laid_out(tiles, dim):
    tiles = jnp.moveaxis(tiles, 0, dim)
    dims = tiles.shape
    return tiles.reshape(*dims[:dim], dims[dim] * dims[dim + 1], *dims[dim + 2 :])


def gathered_copies(shard, axis, dim):
    tiles = sent_to_all(shard, axis)
    return laid_out(tiles, dim)


def sent_together(arrays, axis, split_dim, concat_dim, along):
    ends, at = ([], 0)
    for a in arrays[:-1]:
        at += a.shape[along]
        ends.append(at)
    both = jnp.concatenate(arrays, axis=along)
    return tuple(
        jnp.split(
            lax.all_to_all(both, axis, split_axis=split_dim, concat_axis=concat_dim, tiled=True),
            ends,
            axis=along,
        )
    )


def by_axis(shard, axes):
    return functools.reduce(lax.psum, axes, shard)


def phase_pair(points, lattice, weights):
    winding = (
        points[0][:, None] * lattice[0][None, :]
        + points[1][:, None] * lattice[1][None, :]
        + points[2][:, None] * lattice[2][None, :]
    )
    winding = jnp.mod(winding, GRID)
    angle = 2.0 * math.pi / GRID * winding.astype(jnp.float32)
    inverse = 1.0 / weights.astype(jnp.float32)
    cosine = (jnp.cos(angle) * inverse[None, :]).astype(jnp.bfloat16)
    sine = (jnp.sin(angle) * inverse[None, :]).astype(jnp.bfloat16)
    return (cosine, sine)


def mix_table(table, block):
    return jnp.einsum("kr,nrx->nkx", table, block, preferred_element_type=jnp.float32)


def make_fold(points, lattice, weights):

    def accumulate(carry, piece, start):
        cosine, sine = phase_pair(points, lattice, weights)
        half = piece.shape[2] // 2
        real_in = piece[:, :, :half]
        imag_in = piece[:, :, half:]
        real_out = mix_table(cosine, real_in) - mix_table(sine, imag_in)
        imag_out = mix_table(cosine, imag_in) + mix_table(sine, real_in)
        return jnp.concatenate([real_out, imag_out], axis=1)

    return accumulate


def density_terms(rot_real, rot_imag):
    ham_real = rot_real[0]
    ham_imag = rot_imag[0]
    conn_real = rot_real[1:]
    conn_imag = rot_imag[1:]
    levels = jnp.diagonal(ham_real, axis1=1, axis2=2).astype(jnp.float32)
    filled = jax.nn.sigmoid(-levels / SMEARING)
    vacant = 1.0 - filled

    def multiply(left, right):
        return jnp.einsum("knm,bkml->bknl", left, right, preferred_element_type=jnp.float32)

    prod_real = multiply(ham_real, conn_real) - multiply(ham_imag, conn_imag)
    prod_imag = multiply(ham_real, conn_imag) + multiply(ham_imag, conn_real)
    weight = filled[None, :, :, None] * vacant[None, :, None, :]
    left_real = conn_real.astype(jnp.float32) * weight
    left_imag = conn_imag.astype(jnp.float32) * weight
    traces = jnp.einsum("aknm,bkmn->abk", left_real, prod_imag) + jnp.einsum(
        "aknm,bkmn->abk", left_imag, prod_real
    )
    density = jnp.stack(
        [traces[1, 2] - traces[2, 1], traces[2, 0] - traces[0, 2], traces[0, 1] - traces[1, 0]]
    )
    return density / W


def per_device(kgrid, rvec, degen, operators, vectors):
    own = kgrid.shape[1]
    entries = vectors.shape[1] // 2
    count_ka = lax.axis_size(KA)
    count_op = lax.axis_size("op")
    count_row = lax.axis_size("row")
    count_all = own * count_ka * count_op * count_row
    points = gathered_copies(kgrid, "op", 1)
    folder = make_fold(points, rvec, degen)
    points_count = points.shape[1]
    zeroed = jnp.zeros((1, 2 * points_count, entries), jnp.float32)
    summed = folder(zeroed, lax.all_gather(operators, KA_ROW, axis=1, tiled=True), jnp.int32(0))
    real_k = summed[:, :points_count].astype(jnp.bfloat16)
    imag_k = summed[:, points_count:].astype(jnp.bfloat16)
    real_k, imag_k = sent_together((real_k, imag_k), "op", 1, 0, 2)
    halves = vectors.reshape(own, 2, W, W)
    vec_real = halves[:, 0]
    vec_imag = halves[:, 1]

    def apply_right(left, right):
        return jnp.einsum("kij,kjn->kin", left, right, preferred_element_type=jnp.float32)

    def apply_left(left, right):
        return jnp.einsum("kin,kim->knm", left, right, preferred_element_type=jnp.float32)

    def rotate(block):
        op_real, op_imag = block
        prod_real = (apply_right(op_real, vec_real) - apply_right(op_imag, vec_imag)).astype(
            jnp.bfloat16
        )
        prod_imag = (apply_right(op_real, vec_imag) + apply_right(op_imag, vec_real)).astype(
            jnp.bfloat16
        )
        rot_real = (apply_left(vec_real, prod_real) + apply_left(vec_imag, prod_imag)).astype(
            jnp.bfloat16
        )
        rot_imag = (apply_left(vec_real, prod_imag) - apply_left(vec_imag, prod_real)).astype(
            jnp.bfloat16
        )
        return (rot_real, rot_imag)

    rot_real, rot_imag = lax.map(
        rotate, (real_k.reshape(4, own, W, W), imag_k.reshape(4, own, W, W))
    )
    density = density_terms(rot_real, rot_imag)
    magnetization = by_axis(jnp.sum(density, axis=1), KA_OP_ROW) / count_all
    return (density, magnetization)


def solution(mesh):
    split = Mesh(
        mesh.devices.reshape(8, 2, mesh.shape["op"], mesh.shape["row"]),
        ("ka_0", "ka_1", "op", "row"),
    )
    placed = (P(None, KA_OP_ROW), P(), P(), P("op", KA_ROW, None), P(KA_OP_ROW, None))
    return jax.shard_map(
        per_device,
        mesh=split,
        in_specs=placed,
        out_specs=(P(None, KA_OP_ROW), P()),
        check_vma=False,
    )
```

profile of v0, /device:TPU:1, one launch (start us, length us, event | category | flops | bytes accessed | tf_op | source)
XLA Modules:
  0.0 227.7 jit_solution(6440911563095672124)
XLA Ops:
  7.2 1.5 copy.65
  8.8 1.3 broadcast_in_dim.13
  10.0 4.8 %all-to-all-start = ((s32[4,3,8]{2,1,0:T(4,128)}), s32[4,3,8]{2,1,0:T(4,128)S(1)}, u32[]{:S(2)}, u32[]{:S(2)}) async-start(s32[4,3,8]{2,1,0:T(4,128)} %broadcast_in_dim.13), calls=%async_computation | async-start | bytes 16384 | tf_op jit(solution)/shard_map/all_to_all | solution.py:22
  14.9 0.8 fusion.81
  15.7 0.7 convert_divide_fusion
  16.3 2.7 %all-to-all-done = s32[4,3,8]{2,1,0:T(4,128)S(1)} async-done(((s32[4,3,8]{2,1,0:T(4,128)}), s32[4,3,8]{2,1,0:T(4,128)S(1)}, u32[]{:S(2)}, u32[]{:S(2)}) %all-to-all-start) | async-done | bytes 416 | tf_op jit(solution)/shard_map/all_to_all | solution.py:22
  19.3 90.1 %all-gather.2.cloned.1.call-done = bf16[1,256,12800]{2,0,1:T(2,128)(2,1)} async-done(((bf16[1,2,12800]{2,0,1:T(2,128)(2,1)}), bf16[1,256,12800]{2,0,1:T(2,128)(2,1)}) %all-gather.2.cloned.1.call-update) | async-done | bytes 6553616 | tf_op jit(solution)/shard_map/all_gather | solution.py:126
  109.4 14.6 %fusion.79 = (bf16[1,256,6400]{2,0,1:T(2,128)(2,1)S(1)}, bf16[1,256,6400]{2,0,1:T(2,128)(2,1)S(1)}) fusion(bf16[1,256,12800]{2,0,1:T(2,128)(2,1)} %all-gather.2.cloned.1.call-done), kind=kLoop, calls=%fused_computation.108 | loop fusion | bytes 13107200 | tf_op jit(solution)/shard_map/slice | solution.py:80
  124.1 0.9 fusion.32
  124.9 0.9 fusion.33
  125.8 0.9 fusion.25
  126.7 0.9 fusion.24
  127.7 1.3 copy.123
  129.0 0.5 broadcast.126
  129.5 5.6 %reduce.18 = bf16[32,12800]{1,0:T(8,128)(2,1)S(1)} reduce(bf16[32,1,12800]{2,1,0:T(2,128)(2,1)S(1)} %bitcast.148, bf16[]{:T(256)} %broadcast.126), dimensions={1}, to_apply=%bitcast.111.reduce_sub_computation | reduce | bytes 1638402
  135.1 1.1 reshape.158
  136.2 4.4 %all-to-all-start.1 = ((bf16[4,2,51200]{2,1,0:T(2,128)(2,1)}), bf16[4,2,51200]{2,1,0:T(2,128)(2,1)}, u32[]{:S(2)}, u32[]{:S(2)}) async-start(bf16[4,2,51200]{2,1,0:T(2,128)(2,1)} %reshape.158), calls=%async_computation.1 | async-start | bytes 1638400 | tf_op jit(solution)/shard_map/all_to_all | solution.py:46
  140.6 0.4 reshape.126
  141.0 11.8 %all-to-all-done.1 = bf16[4,2,51200]{2,1,0:T(2,128)(2,1)} async-done(((bf16[4,2,51200]{2,1,0:T(2,128)(2,1)}), bf16[4,2,51200]{2,1,0:T(2,128)(2,1)}, u32[]{:S(2)}, u32[]{:S(2)}) %all-to-all-start.1) | async-done | bytes 819232 | tf_op jit(solution)/shard_map/all_to_all | solution.py:46
  152.8 2.5 %reshape.159 = bf16[32,1,12800]{2,1,0:T(2,128)(2,1)S(1)} reshape(bf16[4,2,51200]{2,1,0:T(2,128)(2,1)} %all-to-all-done.1) | data formatting | bytes 1638400
  155.4 1.1 reshape.125
  156.5 1.1 reshape.127
  157.6 7.8 %while.12 = (s32[]{:T(128)}, bf16[4,8,80,80]{2,3,1,0:T(8,128)(2,1)S(1)}, bf16[4,8,80,80]{2,3,1,0:T(8,128)(2,1)S(1)}, bf16[4,8,80,80]{3,2,1,0:T(8,128)(2,1)S(1)},...) while((s32[]{:T(128)}, ...), condition=%wide.region_1.2_spmd, body=%wide.region_0.1_spmd.sunk | while | flops 65945600 | bytes 5038189 | solution.py:156
  158.8 0.3 fusion.147
  159.3 0.3 fusion.145
  160.8 0.3 fusion.147
  161.3 0.3 fusion.145
  162.7 0.3 fusion.147
  163.2 0.3 fusion.145
  165.5 0.3 copy.70
  165.8 0.3 fusion.46
  166.1 1.6 copy.73
  167.7 3.7 %gather_fusion = bf16[80,8]{1,0:T(8,128)(2,1)S(1)} fusion(bf16[8,80,80]{0,2,1:T(8,128)(2,1)} %copy.73, s32[80]{0:T(128)S(1)} %or_bitcast_fusion), kind=kCustom, calls=%fused_computation | custom fusion | bytes 3200 | tf_op jit(solution)/shard_map/jit(diagonal)/gather | solution.py:94
  171.5 1.1 copy.72
  172.6 1.2 fusion.48
  173.9 1.2 fusion.26
  175.1 0.5 copy.77
  175.8 1.0 convert_multiply_fusion
  176.7 1.2 fusion.27
  178.0 0.5 copy.75
  178.5 1.9 fusion.34
  180.3 0.5 fusion.43
  181.1 0.7 fusion.78
  181.8 12.5 %psum.28 = f32[3]{0:T(128)S(1)} all-reduce(f32[3]{0:T(128)S(1)} %get-tuple-element.62), channel_id=1, replica_groups=mesh['ka_0'=8,'ka_1'=2,'op'=4,'row'=8] {'ka_0'}, use_global_device_ids=true, to_apply=%region_3.4 | all-reduce | flops 3 | bytes 24 | tf_op jit(solution)/shard_map/psum | solution.py:54
  194.3 6.8 %psum.29 = f32[3]{0:T(128)S(1)} all-reduce(f32[3]{0:T(128)S(1)} %psum.28), channel_id=1, replica_groups=mesh['ka_0'=8,'ka_1'=2,'op'=4,'row'=8] {'ka_1'}, use_global_device_ids=true, to_apply=%region_4.5 | all-reduce | flops 3 | bytes 24 | tf_op jit(solution)/shard_map/psum | solution.py:54
  201.1 6.8 %psum.30 = f32[3]{0:T(128)S(1)} all-reduce(f32[3]{0:T(128)S(1)} %psum.29), channel_id=1, replica_groups=mesh['ka_0'=8,'ka_1'=2,'op'=4,'row'=8] {'op'}, use_global_device_ids=true, to_apply=%region_5.6 | all-reduce | flops 3 | bytes 24 | tf_op jit(solution)/shard_map/psum | solution.py:54
  207.9 12.4 %psum.31 = f32[3]{0:T(128)S(1)} all-reduce(f32[3]{0:T(128)S(1)} %psum.30), channel_id=1, replica_groups=mesh['ka_0'=8,'ka_1'=2,'op'=4,'row'=8] {'row'}, use_global_device_ids=true, to_apply=%region_6.7 | all-reduce | flops 3 | bytes 24 | tf_op jit(solution)/shard_map/psum | solution.py:54
  220.3 0.5 broadcast_multiply_fusion.1
  (49 shorter events, 7.0 us)
Async XLA Ops:
  7.2 102.3 %all-gather.2.cloned.1.call-start = ((), (), s32[]{:S(2)}) async-start(), calls=%async_computation.2 | async-start | bytes 13209600 | tf_op jit(solution)/shard_map/all_gather | solution.py:126
  10.0 9.0 %all-to-all-start = ((s32[4,3,8]{2,1,0:T(4,128)}), s32[4,3,8]{2,1,0:T(4,128)S(1)}, u32[]{:S(2)}, u32[]{:S(2)}) async-start(s32[4,3,8]{2,1,0:T(4,128)} %broadcast_in_dim.13), calls=%async_computation | async-start | bytes 16384 | tf_op jit(solution)/shard_map/all_to_all | solution.py:22
  129.0 11.6 %copy-start.1 = (bf16[8,12800]{1,0:T(8,128)(2,1)S(1)}, bf16[8,12800]{1,0:T(8,128)(2,1)}, u32[]{:S(2)}) copy-start(bf16[8,12800]{1,0:T(8,128)(2,1)} %param.11) | copy-start | bytes 614404
  136.2 16.6 %all-to-all-start.1 = ((bf16[4,2,51200]{2,1,0:T(2,128)(2,1)}), bf16[4,2,51200]{2,1,0:T(2,128)(2,1)}, u32[]{:S(2)}, u32[]{:S(2)}) async-start(bf16[4,2,51200]{2,1,0:T(2,128)(2,1)} %reshape.158), calls=%async_computation.1 | async-start | bytes 1638400 | tf_op jit(solution)/shard_map/all_to_all | solution.py:46
  175.1 1.7 copy-start
Sparse Core Ops, SparseCore 0:
  11.2 98.2 all-gather.1
where the time goes:
time: 232 us; the launch traced here: 228 us
  waiting for transfers between devices  105 us (45%)
  blocking collectives  38.5 us (17%)
  local copies, waits for them, and re-layouts  34.5 us (15%)
  matrix products  17.4 us (7%)
  between operations  14.3 us (6%)
  starting transfers between devices  9.24 us (4%)
  other arithmetic  8.93 us (4%)
    all_gather x1, waiting for transfers between devices, per_device(): lax.all_gather(operators, KA_ROW, axis=1, tiled=True)  90.1 us
    psum x4, blocking collectives, by_axis(): return functools.reduce(lax.psum, axes, shard)  38.5 us
    slice x1, local copies, waits for them, and re-layouts, accumulate(): real_in = piece[:, :, :half]  14.6 us
    all_to_all x1, waiting for transfers between devices, sent_together(): lax.all_to_all(both, axis, split_axis=split_dim, concat_axis=concat_dim,...  11.8 us
    unnamed x9, local copies, waits for them, and re-layouts  5.71 us
    unnamed x1, other arithmetic  5.59 us
    all_to_all x1, starting transfers between devices, sent_to_all(): lax.all_to_all(jnp.broadcast_to(shard[None], (count, *shard.shape)), axis...  4.83 us
  transfers between devices with their start and end apart: 3, of which 3 were waited for; matrix products, arithmetic and copies ran while one was open for 2% of the time, Pallas kernels for 0%

commit v1 on v0

v1 whole, which is shorter than its diff:
```python
import functools
import math

import jax
import jax.numpy as jnp
from jax import lax
from jax.experimental import pallas as pl
from jax.experimental.pallas import tpu as pltpu
from jax.sharding import PartitionSpec as P

W = 80
GRID = 64
SMEARING = 0.5
NX, NY, NZ, NC = 4, 8, 8, 2
XC = NX * NC
RING = 8
KPT = 8
NR = 256
HALF = W * W
CHUNK = 256
CHUNKS = HALF // CHUNK
FIRST_Q = 13
KPOINTS = 4096
MESH = pl.DeviceIdType.MESH
BF = jnp.bfloat16
F32 = jnp.float32


def place():
    ka = lax.axis_index("ka")
    return lax.axis_index("op"), lax.div(ka, 2), lax.rem(ka, 2), lax.axis_index("row")


def at(x, y, c, z):
    return (2 * y + c, x, z)


def held_p(c, z):
    live = (c == 0) | (lax.rem(z, 2) == 0) | (z == 7)
    return live, jnp.where(c == 0, z, 8 + lax.div(z + 1, 2))


def held_q(c, y):
    live = (c == 1) | (lax.rem(y, 2) == 0)
    return live, FIRST_Q + jnp.where(c == 1, y, 8 + lax.div(y, 2))


def settle(ref, sem):
    pltpu.make_async_copy(ref, ref, sem).wait()


def push(src, dst, send_sem, recv_sem, device):
    pltpu.make_async_remote_copy(
        src_ref=src, dst_ref=dst, send_sem=send_sem, recv_sem=recv_sem,
        device_id=device, device_id_type=MESH,
    ).start()


def keep(src, dst, sem):
    pltpu.make_async_copy(src, dst, sem).start()


def each(count, body):
    def step(i, carry):
        body(i)
        return carry

    lax.fori_loop(0, count, step, 0)


def iota(shape, dim):
    return lax.broadcasted_iota(jnp.int32, shape, dim)


def dot(a, b):
    return jnp.dot(a, b, preferred_element_type=F32)


def matrix_rows(tile, put):
    lane = iota((KPT, 128), 1)
    for i in range(W):
        first, off = divmod(i * W, 128)
        row = tile(first)
        if off:
            row = pltpu.roll(row, 128 - off, 1)
            if off + W > 128:
                nxt = pltpu.roll(tile(first + 1), 128 - off, 1)
                row = jnp.where(lane < 128 - off, row, nxt)
        put(i, jnp.where(lane < W, row, 0.0))


def fold_table(rows_ref, lattice, inverse, table):
    points = rows_ref[:, 0, :]
    spread = (lax.div(iota((512, 64), 0), 8) == iota((512, 64), 1)).astype(F32).astype(BF)
    wide = dot(spread, points.astype(BF))
    own = lax.rem(iota((512, 128), 0), 8) == lax.rem(iota((512, 128), 1), 8)
    wide = jnp.where(own, wide, 0.0).astype(BF)
    for part in range(4):
        winding = dot(wide[part * 128:(part + 1) * 128], lattice)
        winding = winding - GRID * jnp.floor(winding * (1.0 / GRID))
        upper = winding >= GRID // 2
        turn = jnp.where(upper, winding - (GRID // 2), winding) - (GRID // 4)
        sign = jnp.where(upper, -inverse, inverse)
        angle = turn * (2.0 * math.pi / GRID)
        sq = angle * angle
        odd = -1.0 / 39916800.0
        for term in (1.0 / 362880.0, -1.0 / 5040.0, 1.0 / 120.0, -1.0 / 6.0, 1.0):
            odd = odd * sq + term
        even = 1.0 / 479001600.0
        for term in (-1.0 / 3628800.0, 1.0 / 40320.0, -1.0 / 720.0, 1.0 / 24.0, -0.5, 1.0):
            even = even * sq + term
        table[part * 128:(part + 1) * 128, :NR] = (-odd * angle * sign).astype(BF)
        table[part * 128:(part + 1) * 128, NR:] = (even * sign).astype(BF)


def transform(table, gathered, out):
    for part in range(4):
        rows = slice(part * 128, (part + 1) * 128)
        block = gathered[...].reshape(NR, 2 * CHUNK)
        turned = jnp.concatenate([-block[:, CHUNK:], block[:, :CHUNK]], axis=1)
        total = dot(table[rows, :NR], block) + dot(table[rows, NR:], turned)
        out[part * 16:(part + 1) * 16] = total.reshape(16, KPT, 2 * CHUNK).astype(BF)


def body(
    kgrid, rvec, degen, operators, vectors, density, magnet,
    vec, own_row, k_p, k_q, in_p, in_q, stage, all_p, all_q, tab_p, tab_q,
    out_p, out_q, full, mats, right, left, sums,
    send1, send2, send3, k1_sem, k2_sem, in_sem, all_sem, full_sem, vec_sem, sum_send, sum_sem,
):
    x, y, c, z = place()
    xc = 2 * x + c
    live_p, chunk_p = held_p(c, z)
    live_q, chunk_q = held_q(c, y)
    barrier = pltpu.get_barrier_semaphore()
    keep(vectors, vec, vec_sem)

    def greet(i):
        px, pc, ring = lax.div(i, 16), lax.rem(lax.div(i, 8), 2), lax.rem(i, 8)
        same = (px == x) & (pc == c)

        @pl.when(jnp.logical_not(same & (ring == z)))
        def _():
            pl.semaphore_signal(barrier, inc=1, device_id=at(px, y, pc, ring), device_id_type=MESH)

        @pl.when(ring != y)
        def _():
            pl.semaphore_signal(barrier, inc=1, device_id=at(px, ring, pc, z), device_id_type=MESH)

    each(64, greet)

    stage[...] = jnp.zeros_like(stage)
    stage[0:3, 0:KPT] = kgrid[...].astype(F32)
    row = stage[0:1, 0:128]
    row = row + pltpu.roll(stage[1:2, 0:128], 8, 1) + pltpu.roll(stage[2:3, 0:128], 16, 1)
    own_row[0] = row
    k_p[xc * 8 + z] = row
    k_q[xc * 8 + y] = row

    pl.semaphore_wait(barrier, 63 + 56)

    def share_points(i):
        @pl.when(i != z)
        def _():
            push(own_row.at[0], k_p.at[xc * 8 + z], send1, k1_sem.at[0], at(x, y, c, i))

        @pl.when(i != y)
        def _():
            push(own_row.at[0], k_q.at[xc * 8 + y], send1, k1_sem.at[1], at(x, i, c, z))

    each(RING, share_points)

    def pieces(chunk, dst, sem, device, local):
        for part in range(2):
            col = pl.multiple_of(part * HALF + chunk * CHUNK, 128)
            src = operators.at[0, :, pl.ds(col, CHUNK)]
            if local:
                keep(src, dst.at[part], sem)
            else:
                push(src, dst.at[part], send2, sem, device)

    def share_columns(i):
        pc, ring = lax.div(i, 8), lax.rem(i, 8)
        live, chunk = held_p(pc, ring)
        me = (pc == c) & (ring == z)

        @pl.when(live & me)
        def _():
            pieces(chunk, in_p.at[c * 8 + z], in_sem.at[0], None, True)

        @pl.when(live & jnp.logical_not(me))
        def _():
            pieces(chunk, in_p.at[c * 8 + z], in_sem.at[0], at(x, y, pc, ring), False)

        live2, chunk2 = held_q(pc, ring)
        me2 = (pc == c) & (ring == y)

        @pl.when(live2 & me2)
        def _():
            pieces(chunk2, in_q.at[c * 8 + y], in_sem.at[1], None, True)

        @pl.when(live2 & jnp.logical_not(me2))
        def _():
            pieces(chunk2, in_q.at[c * 8 + y], in_sem.at[1], at(x, ring, pc, z), False)

    each(16, share_columns)

    settle(k_p.at[pl.ds(0, 7)], k1_sem.at[0])
    settle(k_q.at[pl.ds(0, 7)], k1_sem.at[1])

    def share_rows(i):
        px, pc = lax.div(i, 2), lax.rem(i, 2)

        @pl.when(i != xc)
        def _():
            push(k_p.at[pl.ds(xc * 8, 8)], k_p.at[pl.ds(xc * 8, 8)], send1, k2_sem.at[0], at(px, y, pc, z))
            push(k_q.at[pl.ds(xc * 8, 8)], k_q.at[pl.ds(xc * 8, 8)], send1, k2_sem.at[1], at(px, y, pc, z))

    each(XC, share_rows)

    def collect(incoming, gathered, slot, sem, gather_sem, along_y):
        settle(incoming, sem)
        for s in range(16):
            for part in range(2):
                stage[2 * s:2 * s + 2, part * CHUNK:(part + 1) * CHUNK] = incoming[s, part].astype(F32)
        gathered[slot] = stage[...].astype(BF)

        def spread(i):
            @pl.when(i != slot)
            def _():
                device = at(x, i, c, z) if along_y else at(x, y, c, i)
                push(gathered.at[slot], gathered.at[slot], send3, gather_sem, device)

        each(RING, spread)

    @pl.when(live_p)
    def _():
        collect(in_p, all_p, y, in_sem.at[0], all_sem.at[0], True)

    @pl.when(live_q)
    def _():
        collect(in_q, all_q, z, in_sem.at[1], all_sem.at[1], False)

    pltpu.make_async_copy(vectors, vec, vec_sem).wait()
    for part in range(2):
        def put(i, val, part=part):
            mats[part, i * KPT:(i + 1) * KPT, :] = val

        matrix_rows(lambda t, part=part: vec[:, part * HALF + t * 128: part * HALF + (t + 1) * 128].astype(F32), put)

    lane = iota((W, 128), 1)

    def eigen(k):
        vr = mats[0, pl.ds(k, W, stride=KPT), :]
        vi = mats[1, pl.ds(k, W, stride=KPT), :]
        gap = jnp.zeros((48, 256), BF)
        right[k, 0:W, :] = jnp.concatenate([vr, vi], axis=1).astype(BF)
        right[k, W:128, :] = gap
        right[k, 128:128 + W, :] = jnp.concatenate([-vi, vr], axis=1).astype(BF)
        right[k, 128 + W:, :] = gap
        fill = jnp.zeros((48, 128), F32)
        tr = jnp.transpose(jnp.concatenate([vr, fill], axis=0))[:W]
        ti = jnp.transpose(jnp.concatenate([vi, fill], axis=0))[:W]
        left[k] = paired(tr, ti).astype(BF)

    def paired(re, im):
        moved = pltpu.roll(im, W, 1)
        return jnp.concatenate([jnp.where(lane < W, re, moved), jnp.where(lane < 2 * W - 128, moved, 0.0)], axis=1)

    each(KPT, eigen)

    settle(k_p.at[pl.ds(0, 56)], k2_sem.at[0])
    settle(k_q.at[pl.ds(0, 56)], k2_sem.at[1])
    lattice_rows = iota((128, NR), 0)
    rv = rvec[...].astype(F32)
    lattice = jnp.where(
        lattice_rows < 8, rv[0:1],
        jnp.where(lattice_rows < 16, rv[1:2], jnp.where(lattice_rows < 24, rv[2:3], 0.0)),
    )
    weight = degen[...].astype(F32)

    @pl.when(live_p)
    def _():
        fold_table(k_p, lattice.astype(BF), 1.0 / weight, tab_p)

    @pl.when(live_q)
    def _():
        col = iota((NR, NR), 1)
        source = (
            lax.rem(lax.div(col, 2), 8) * 32 + lax.rem(lax.div(col, 16), 2) * 16
            + lax.div(col, 32) * 2 + lax.rem(col, 2)
        )
        swap = (iota((NR, NR), 0) == source).astype(F32).astype(BF)
        moved = dot(lattice.astype(BF), swap).astype(BF)
        weights = dot(jnp.broadcast_to(weight, (8, NR)).astype(BF), swap)[0:1]
        fold_table(k_q, moved, 1.0 / weights, tab_q)

    def deliver(chunk, out, along_z):
        def one(i):
            px, pc, ring = lax.div(i, 16), lax.rem(lax.div(i, 8), 2), lax.rem(i, 8)
            me = (px == x) & (pc == c) & (ring == (z if along_z else y))
            dst = full.at[x, chunk]
            device = at(px, y, pc, ring) if along_z else at(px, ring, pc, z)

            @pl.when(me)
            def _():
                keep(out.at[i], dst, full_sem)

            @pl.when(jnp.logical_not(me))
            def _():
                push(out.at[i], dst, send3, full_sem, device)

        each(64, one)

    @pl.when(live_p)
    def _():
        settle(all_p.at[pl.ds(0, 7)], all_sem.at[0])
        transform(tab_p, all_p, out_p)
        deliver(chunk_p, out_p, True)

    @pl.when(live_q)
    def _():
        settle(all_q.at[pl.ds(0, 7)], all_sem.at[1])
        transform(tab_q, all_q, out_q)
        deliver(chunk_q, out_q, False)

    settle(full, full_sem)

    def rebuild(o):
        for part in range(2):
            def put(i, val, part=part):
                mats[2 * o + part, i * KPT:(i + 1) * KPT, :] = val

            matrix_rows(
                lambda t, part=part: full[o, t // 2, :, part * CHUNK + (t % 2) * 128: part * CHUNK + (t % 2 + 1) * 128].astype(F32),
                put,
            )

    each(4, rebuild)

    sub = iota((W, 128), 0)
    density_lane = iota((1, 128), 1)

    def point(k, carry):
        ops = [
            jnp.concatenate(
                [mats[2 * o, pl.ds(k, W, stride=KPT), :], mats[2 * o + 1, pl.ds(k, W, stride=KPT), :]], axis=1
            ).astype(BF)
            for o in range(4)
        ]
        prod = dot(jnp.concatenate(ops, axis=0), right[k])
        turn = left[k][:, :256]
        rot = []
        for o in range(4):
            re = prod[o * W:(o + 1) * W, :128]
            im = prod[o * W:(o + 1) * W, 128:]
            stacked = jnp.concatenate(
                [jnp.concatenate([re, im], axis=1), jnp.concatenate([im, -re], axis=1), jnp.zeros((96, 256), F32)],
                axis=0,
            ).astype(BF)
            rot.append(dot(turn, stacked).astype(BF).astype(F32))
        ham_re, ham_im = rot[0][:, :128], rot[0][:, 128:]
        diag = jnp.where(sub == lane, ham_re, 0.0)
        down = 1.0 / (1.0 + jnp.exp(jnp.sum(diag, axis=1, keepdims=True) * (1.0 / SMEARING)))
        along = 1.0 / (1.0 + jnp.exp(jnp.sum(diag, axis=0, keepdims=True) * (1.0 / SMEARING)))
        weight2 = (1.0 - down) * along
        ham = paired(ham_re, ham_im).astype(BF)
        prods, turned = [], []
        fill = jnp.zeros((48, 128), F32)
        for b in range(3):
            re, im = rot[b + 1][:, :128], rot[b + 1][:, 128:]
            stacked = jnp.concatenate(
                [jnp.concatenate([re, im], axis=1), jnp.concatenate([-im, re], axis=1), jnp.zeros((96, 256), F32)],
                axis=0,
            ).astype(BF)
            prods.append(dot(ham, stacked))
            turned.append((
                jnp.transpose(jnp.concatenate([re, fill], axis=0))[:W] * weight2,
                jnp.transpose(jnp.concatenate([im, fill], axis=0))[:W] * weight2,
            ))
        for comp, (a, b) in enumerate(((1, 2), (2, 0), (0, 1))):
            terms = (
                turned[a][0] * prods[b][:, 128:] + turned[a][1] * prods[b][:, :128]
                - turned[b][0] * prods[a][:, 128:] - turned[b][1] * prods[a][:, :128]
            )
            total = jnp.sum(jnp.sum(terms, axis=0, keepdims=True), axis=1, keepdims=True) * (1.0 / W)
            stage[comp:comp + 1, 0:128] = stage[comp:comp + 1, 0:128] + jnp.where(density_lane == k, total, 0.0)
        return carry

    stage[0:8, 0:128] = jnp.zeros((8, 128), F32)
    lax.fori_loop(0, KPT, point, 0)
    dens = stage[0:8, 0:128]
    density[...] = dens[0:3, 0:KPT]

    total = jnp.sum(dens, axis=1, keepdims=True)
    eye = iota((8, 128), 0) == iota((8, 128), 1)
    part = jnp.sum(jnp.where(eye, total, 0.0), axis=0, keepdims=True)
    for level in range(3):
        slot = (xc, z, y)[level]
        sums[level, slot] = part

        def tell(i, level=level, slot=slot):
            px, pc = lax.div(i, 2), lax.rem(i, 2)
            device = (at(px, y, pc, z), at(x, y, c, i), at(x, i, c, z))[level]

            @pl.when(i != slot)
            def _():
                push(sums.at[level, slot], sums.at[level, slot], sum_send, sum_sem.at[level], device)

        each(8, tell)
        settle(sums.at[level, pl.ds(0, 7)], sum_sem.at[level])
        part = jnp.sum(sums[level, :, 0, :], axis=0, keepdims=True)
    magnet[...] = part[:, 0:3] * (1.0 / KPOINTS)

    for level in range(3):
        settle(sums.at[level, pl.ds(0, 7)], sum_send)
    settle(k_p.at[pl.ds(0, 14)], send1)
    settle(k_p.at[pl.ds(0, 56)], send1)
    settle(k_p.at[pl.ds(0, 56)], send1)

    settle(in_p.at[pl.ds(0, 12)], send2)

    @pl.when(jnp.logical_not(live_p))
    def _():
        settle(in_p.at[pl.ds(0, 1)], send2)

    settle(in_q.at[pl.ds(0, 11)], send2)

    @pl.when(jnp.logical_not(live_q))
    def _():
        settle(in_q.at[pl.ds(0, 1)], send2)

    @pl.when(live_p)
    def _():
        settle(all_p.at[pl.ds(0, 7)], send3)
        settle(out_p.at[pl.ds(0, 63)], send3)

    @pl.when(live_q)
    def _():
        settle(all_q.at[pl.ds(0, 7)], send3)
        settle(out_q.at[pl.ds(0, 63)], send3)


def per_device(kgrid, rvec, degen, operators, vectors):
    vmem = pl.BlockSpec(memory_space=pltpu.VMEM)
    anywhere = pl.BlockSpec(memory_space=pl.ANY)
    dma = pltpu.SemaphoreType.DMA
    density, magnet = pl.pallas_call(
        body,
        out_shape=(jax.ShapeDtypeStruct((3, KPT), F32), jax.ShapeDtypeStruct((1, 3), F32)),
        in_specs=[vmem, vmem, vmem, anywhere, anywhere],
        out_specs=(vmem, vmem),
        scratch_shapes=[
            pltpu.VMEM((KPT, 2 * HALF), BF),
            pltpu.VMEM((1, 1, 128), F32),
            pltpu.VMEM((64, 1, 128), F32),
            pltpu.VMEM((64, 1, 128), F32),
            pltpu.VMEM((16, 2, 2, CHUNK), BF),
            pltpu.VMEM((16, 2, 2, CHUNK), BF),
            pltpu.VMEM((32, 2 * CHUNK), F32),
            pltpu.VMEM((RING, 32, 2 * CHUNK), BF),
            pltpu.VMEM((RING, 32, 2 * CHUNK), BF),
            pltpu.VMEM((512, 2 * NR), BF),
            pltpu.VMEM((512, 2 * NR), BF),
            pltpu.VMEM((64, KPT, 2 * CHUNK), BF),
            pltpu.VMEM((64, KPT, 2 * CHUNK), BF),
            pltpu.VMEM((4, CHUNKS, KPT, 2 * CHUNK), BF),
            pltpu.VMEM((8, W * KPT, 128), F32),
            pltpu.VMEM((KPT, 256, 256), BF),
            pltpu.VMEM((KPT, W, 256), BF),
            pltpu.VMEM((3, 8, 1, 128), F32),
            dma, dma, dma, dma((2,)), dma((2,)), dma((2,)), dma((2,)), dma, dma, dma, dma((3,)),
        ],
        compiler_params=pltpu.CompilerParams(
            collective_id=0, has_side_effects=True, vmem_limit_bytes=56 * 1024 * 1024
        ),
        name="orbital",
    )(kgrid, rvec, degen.reshape(1, NR), operators, vectors)
    return density, magnet.reshape(3)


def solution(mesh):
    return jax.shard_map(
        per_device,
        mesh=mesh,
        in_specs=(P(None, ("ka", "op", "row")), P(), P(), P("op", ("ka", "row"), None), P(("ka", "op", "row"), None)),
        out_specs=(P(None, ("ka", "op", "row")), P()),
        check_vma=False,
    )
```

time: 232 us -> 66.2 us (0.29); the launches traced: 228 us -> 65.3 us
  waiting for transfers between devices: 105 us -> 0 us
  Pallas kernels: 0 us -> 62.8 us
  blocking collectives: 38.5 us -> 0 us
  local copies, waits for them, and re-layouts: 34.5 us -> 1.8 us
  matrix products: 17.4 us -> 0 us
  between operations: 14.3 us -> 0.65 us
  starting transfers between devices: 9.24 us -> 0 us
  other arithmetic: 8.93 us -> 0 us
    all_gather x1 -> x0, waiting for transfers between devices: 90.1 us -> none  [per_device(): lax.all_gather(operators, KA_ROW, axis=1, tiled=True)]
    pallas_call x0 -> x1, Pallas kernels: none -> 62.8 us  [per_device(): pl.pallas_call(body, out_shape=(jax.ShapeDtypeStruct((3, KPT), F32), jax....]
    psum x4 -> x0, blocking collectives: 38.5 us -> none  [by_axis(): return functools.reduce(lax.psum, axes, shard)]
    dot_general x42 -> x0, matrix products: 17.4 us -> none  [the longest x16 4.07 us: apply_left(): jnp.einsum('kin,kim->knm', left, right, preferred_element_type=jnp.float32)]
    slice x3 -> x0, local copies, waits for them, and re-layouts: 15.5 us -> none  [the longest x1 14.6 us: accumulate(): real_in = piece[:, :, :half]]
    all_to_all x2 -> x0, waiting for transfers between devices: 14.5 us -> none  [the longest x1 11.8 us: sent_together(): lax.all_to_all(both, axis, split_axis=split_dim, concat_axis=concat_dim,...]
    all_to_all x2 -> x0, starting transfers between devices: 9.2 us -> none  [the longest x1 4.83 us: sent_to_all(): lax.all_to_all(jnp.broadcast_to(shard[None], (count, *shard.shape)), axis...]
    unnamed x1 -> x0, other arithmetic: 5.59 us -> none
  transfers between devices with their start and end apart: 3 -> 0, of which waited for: 3 -> 0; matrix products, arithmetic and copies ran while one was open for 2% -> 0% of each run, Pallas kernels for 0% -> 0%
where the time goes in v1:
time: 66.2 us; the launch traced here: 65.3 us
  Pallas kernels  62.8 us (95%)
  local copies, waits for them, and re-layouts  1.8 us (3%)
    pallas_call x1, Pallas kernels, per_device(): pl.pallas_call(body, out_shape=(jax.ShapeDtypeStruct((3, KPT), F32), jax....  62.8 us
    unnamed x6, local copies, waits for them, and re-layouts  1.8 us

profile of v1, /device:TPU:1, one launch (start us, length us, event | category | flops | bytes accessed | tf_op | source)
XLA Modules:
  0.0 65.3 jit_solution(18187899847063458555)
XLA Ops:
  0.6 62.8 %orbital.1 = (f32[3,8]{1,0:T(4,128)}, f32[1,3]{1,0:T(1,128)}) custom-call(s32[3,8]{1,0:T(4,128)} %kgrid.1, s32[3,256]{1,0:T(4,128)} %rvec.1, s32[1,256]{1,0:T(1,128)} %bitcast.2, bf16[1,2,12800]{2,1,0:T(2,128)(2,1)} %operators.1, bf16[8,12800]{1,0:T(8,128)(2,1)} %vectors.1), custom_call_target="tpu_custom_call" | custom-call | tf_op jit(solution)/shard_map/orbital/pallas_call | solution.py:448
  63.5 0.0 copy-start
  63.5 0.7 %copy-done = f32[3,8]{1,0:T(4,128)S(1)} copy-done((f32[3,8]{1,0:T(4,128)S(1)}, f32[3,8]{1,0:T(4,128)}, u32[]{:S(2)}) %copy-start) | copy-done | bytes 120
  64.1 0.0 copy-start.1
  64.1 0.6 copy.9
  64.7 0.1 copy-done.1
  64.8 0.5 copy.10
Async XLA Ops:
  63.5 0.7 %copy-start = (f32[3,8]{1,0:T(4,128)S(1)}, f32[3,8]{1,0:T(4,128)}, u32[]{:S(2)}) copy-start(f32[3,8]{1,0:T(4,128)} %get-tuple-element.8) | copy-start | bytes 292
  64.1 0.6 copy-start.1

commit v2 on v1

--- a/solution.py
+++ b/solution.py
@@ -21,6 +21,7 @@
 CHUNKS = HALF // CHUNK
 FIRST_Q = 13
 KPOINTS = 4096
+TOGETHER = 2
 MESH = pl.DeviceIdType.MESH
 BF = jnp.bfloat16
 F32 = jnp.float32
@@ -43,6 +44,9 @@
 def held_q(c, y):
     live = (c == 1) | (lax.rem(y, 2) == 0)
     return live, FIRST_Q + jnp.where(c == 1, y, 8 + lax.div(y, 2))
+
+
+FAR = (4, 3, 5, 2, 6, 1, 7)
 
 
 def settle(ref, sem):
@@ -66,6 +70,19 @@
         return carry
 
     lax.fori_loop(0, count, step, 0)
+
+
+def around(place, step):
+    return lax.rem(place + step, RING)
+
+
+def partners(x, c):
+    order = ((2, 0), (2, 1), (1, 0), (3, 0), (1, 1), (3, 1), (0, 1), (0, 0))
+    found = []
+    for dx, dc in order:
+        px, pc = lax.rem(x + dx, NX), (1 - c if dc else c)
+        found.append((px, pc, 2 * px + pc))
+    return found
 
 
 def iota(shape, dim):
@@ -123,31 +140,31 @@
 
 
 def body(
-    kgrid, rvec, degen, operators, vectors, density, magnet,
-    vec, own_row, k_p, k_q, in_p, in_q, stage, all_p, all_q, tab_p, tab_q,
-    out_p, out_q, full, mats, right, left, sums,
-    send1, send2, send3, k1_sem, k2_sem, in_sem, all_sem, full_sem, vec_sem, sum_send, sum_sem,
+    kgrid_hbm, rvec_hbm, degen_hbm, operators, vectors, density, magnet,
+    kgrid, rvec, degen, vec, own_row, k_p, k_q, in_p, in_q, stage, all_p, all_q, tab_p, tab_q,
+    out_p, out_q, full, mats, right, left, sums, sums2,
+    send1, send2, send3, k1_sem, k2_sem, in_sem, all_sem, full_sem, vec_sem, sum_send, sum_sem, kg_sem, small_sem,
 ):
     x, y, c, z = place()
     xc = 2 * x + c
     live_p, chunk_p = held_p(c, z)
     live_q, chunk_q = held_q(c, y)
     barrier = pltpu.get_barrier_semaphore()
+    keep(kgrid_hbm, kgrid, kg_sem)
+    keep(rvec_hbm, rvec, small_sem.at[0])
+    keep(degen_hbm, degen, small_sem.at[1])
     keep(vectors, vec, vec_sem)
-
-    def greet(i):
-        px, pc, ring = lax.div(i, 16), lax.rem(lax.div(i, 8), 2), lax.rem(i, 8)
-        same = (px == x) & (pc == c)
-
-        @pl.when(jnp.logical_not(same & (ring == z)))
-        def _():
-            pl.semaphore_signal(barrier, inc=1, device_id=at(px, y, pc, ring), device_id_type=MESH)
-
-        @pl.when(ring != y)
-        def _():
-            pl.semaphore_signal(barrier, inc=1, device_id=at(px, ring, pc, z), device_id_type=MESH)
-
-    each(64, greet)
+    columns = partners(x, c)
+
+    def greet(step):
+        for px, pc, _ in columns:
+            pl.semaphore_signal(barrier, inc=1, device_id=at(px, y, pc, around(z, step)), device_id_type=MESH)
+            pl.semaphore_signal(barrier, inc=1, device_id=at(px, around(y, step), pc, z), device_id_type=MESH)
+
+    for px, pc, _ in columns[:-1]:
+        pl.semaphore_signal(barrier, inc=1, device_id=at(px, y, pc, z), device_id_type=MESH)
+    each(7, lambda i: greet(i + 1))
+    pltpu.make_async_copy(kgrid_hbm, kgrid, kg_sem).wait()
 
     stage[...] = jnp.zeros_like(stage)
     stage[0:3, 0:KPT] = kgrid[...].astype(F32)
@@ -159,16 +176,9 @@
 
     pl.semaphore_wait(barrier, 63 + 56)
 
-    def share_points(i):
-        @pl.when(i != z)
-        def _():
-            push(own_row.at[0], k_p.at[xc * 8 + z], send1, k1_sem.at[0], at(x, y, c, i))
-
-        @pl.when(i != y)
-        def _():
-            push(own_row.at[0], k_q.at[xc * 8 + y], send1, k1_sem.at[1], at(x, i, c, z))
-
-    each(RING, share_points)
+    for step in FAR:
+        push(own_row.at[0], k_p.at[xc * 8 + z], send1, k1_sem.at[0], at(x, y, c, around(z, step)))
+        push(own_row.at[0], k_q.at[xc * 8 + y], send1, k1_sem.at[1], at(x, around(y, step), c, z))
 
     def pieces(chunk, dst, sem, device, local):
         for part in range(2):
@@ -179,44 +189,40 @@
             else:
                 push(src, dst.at[part], send2, sem, device)
 
-    def share_columns(i):
-        pc, ring = lax.div(i, 8), lax.rem(i, 8)
+    def offer(step, pc):
+        ring = around(z, step)
         live, chunk = held_p(pc, ring)
-        me = (pc == c) & (ring == z)
-
-        @pl.when(live & me)
-        def _():
-            pieces(chunk, in_p.at[c * 8 + z], in_sem.at[0], None, True)
-
-        @pl.when(live & jnp.logical_not(me))
+
+        @pl.when(live)
         def _():
             pieces(chunk, in_p.at[c * 8 + z], in_sem.at[0], at(x, y, pc, ring), False)
 
-        live2, chunk2 = held_q(pc, ring)
-        me2 = (pc == c) & (ring == y)
-
-        @pl.when(live2 & me2)
+        ring2 = around(y, step)
+        live2, chunk2 = held_q(pc, ring2)
+
+        @pl.when(live2)
         def _():
-            pieces(chunk2, in_q.at[c * 8 + y], in_sem.at[1], None, True)
-
-        @pl.when(live2 & jnp.logical_not(me2))
-        def _():
-            pieces(chunk2, in_q.at[c * 8 + y], in_sem.at[1], at(x, ring, pc, z), False)
-
-    each(16, share_columns)
+            pieces(chunk2, in_q.at[c * 8 + y], in_sem.at[1], at(x, ring2, pc, z), False)
+
+    for step in FAR:
+        offer(step, c)
+        offer(step, 1 - c)
+    offer(0, 1 - c)
+
+    @pl.when(live_p)
+    def _():
+        pieces(chunk_p, in_p.at[c * 8 + z], in_sem.at[0], None, True)
+
+    @pl.when(live_q)
+    def _():
+        pieces(chunk_q, in_q.at[c * 8 + y], in_sem.at[1], None, True)
 
     settle(k_p.at[pl.ds(0, 7)], k1_sem.at[0])
     settle(k_q.at[pl.ds(0, 7)], k1_sem.at[1])
 
-    def share_rows(i):
-        px, pc = lax.div(i, 2), lax.rem(i, 2)
-
-        @pl.when(i != xc)
-        def _():
-            push(k_p.at[pl.ds(xc * 8, 8)], k_p.at[pl.ds(xc * 8, 8)], send1, k2_sem.at[0], at(px, y, pc, z))
-            push(k_q.at[pl.ds(xc * 8, 8)], k_q.at[pl.ds(xc * 8, 8)], send1, k2_sem.at[1], at(px, y, pc, z))
-
-    each(XC, share_rows)
+    for px, pc, _ in columns[:-1]:
+        push(k_p.at[pl.ds(xc * 8, 8)], k_p.at[pl.ds(xc * 8, 8)], send1, k2_sem.at[0], at(px, y, pc, z))
+        push(k_q.at[pl.ds(xc * 8, 8)], k_q.at[pl.ds(xc * 8, 8)], send1, k2_sem.at[1], at(px, y, pc, z))
 
     def collect(incoming, gathered, slot, sem, gather_sem, along_y):
         settle(incoming, sem)
@@ -225,13 +231,9 @@
                 stage[2 * s:2 * s + 2, part * CHUNK:(part + 1) * CHUNK] = incoming[s, part].astype(F32)
         gathered[slot] = stage[...].astype(BF)
 
-        def spread(i):
-            @pl.when(i != slot)
-            def _():
-                device = at(x, i, c, z) if along_y else at(x, y, c, i)
-                push(gathered.at[slot], gathered.at[slot], send3, gather_sem, device)
-
-        each(RING, spread)
+        for step in FAR:
+            device = at(x, around(y, step), c, z) if along_y else at(x, y, c, around(z, step))
+            push(gathered.at[slot], gathered.at[slot], send3, gather_sem, device)
 
     @pl.when(live_p)
     def _():
@@ -265,10 +267,12 @@
 
     def paired(re, im):
         moved = pltpu.roll(im, W, 1)
-        return jnp.concatenate([jnp.where(lane < W, re, moved), jnp.where(lane < 2 * W - 128, moved, 0.0)], axis=1)
+        return jnp.concatenate([jnp.where(lane < W, re, moved), moved[:, :2 * W - 128]], axis=1)
 
     each(KPT, eigen)
 
+    pltpu.make_async_copy(rvec_hbm, rvec, small_sem.at[0]).wait()
+    pltpu.make_async_copy(degen_hbm, degen, small_sem.at[1]).wait()
     settle(k_p.at[pl.ds(0, 56)], k2_sem.at[0])
     settle(k_q.at[pl.ds(0, 56)], k2_sem.at[1])
     lattice_rows = iota((128, NR), 0)
@@ -296,21 +300,21 @@
         fold_table(k_q, moved, 1.0 / weights, tab_q)
 
     def deliver(chunk, out, along_z):
-        def one(i):
-            px, pc, ring = lax.div(i, 16), lax.rem(lax.div(i, 8), 2), lax.rem(i, 8)
-            me = (px == x) & (pc == c) & (ring == (z if along_z else y))
-            dst = full.at[x, chunk]
-            device = at(px, y, pc, ring) if along_z else at(px, ring, pc, z)
-
-            @pl.when(me)
-            def _():
-                keep(out.at[i], dst, full_sem)
-
-            @pl.when(jnp.logical_not(me))
-            def _():
-                push(out.at[i], dst, send3, full_sem, device)
-
-        each(64, one)
+        dst = full.at[x, chunk]
+
+        def one(step, some):
+            ring = around(z if along_z else y, step)
+            for px, pc, pxc in some:
+                device = at(px, y, pc, ring) if along_z else at(px, ring, pc, z)
+                push(out.at[pxc * 8 + ring], dst, send3, full_sem, device)
+
+        def far(i):
+            half = lax.div(i + 1, 2)
+            one(jnp.where(lax.rem(i, 2) == 0, 4 + half, 4 - half), columns)
+
+        each(7, far)
+        one(0, columns[:-1])
+        keep(out.at[xc * 8 + (z if along_z else y)], dst, full_sem)
 
     @pl.when(live_p)
     def _():
@@ -349,13 +353,13 @@
             for o in range(4)
         ]
         prod = dot(jnp.concatenate(ops, axis=0), right[k])
-        turn = left[k][:, :256]
+        turn = left[k]
         rot = []
         for o in range(4):
             re = prod[o * W:(o + 1) * W, :128]
             im = prod[o * W:(o + 1) * W, 128:]
             stacked = jnp.concatenate(
-                [jnp.concatenate([re, im], axis=1), jnp.concatenate([im, -re], axis=1), jnp.zeros((96, 256), F32)],
+                [jnp.concatenate([re, im], axis=1), jnp.concatenate([im, -re], axis=1)],
                 axis=0,
             ).astype(BF)
             rot.append(dot(turn, stacked).astype(BF).astype(F32))
@@ -370,7 +374,7 @@
         for b in range(3):
             re, im = rot[b + 1][:, :128], rot[b + 1][:, 128:]
             stacked = jnp.concatenate(
-                [jnp.concatenate([re, im], axis=1), jnp.concatenate([-im, re], axis=1), jnp.zeros((96, 256), F32)],
+                [jnp.concatenate([re, im], axis=1), jnp.concatenate([-im, re], axis=1)],
                 axis=0,
             ).astype(BF)
             prods.append(dot(ham, stacked))
@@ -388,32 +392,41 @@
         return carry
 
     stage[0:8, 0:128] = jnp.zeros((8, 128), F32)
-    lax.fori_loop(0, KPT, point, 0)
+    def points(i, carry):
+        for j in range(TOGETHER):
+            carry = point(TOGETHER * i + j, carry)
+        return carry
+
+    lax.fori_loop(0, KPT // TOGETHER, points, 0)
     dens = stage[0:8, 0:128]
     density[...] = dens[0:3, 0:KPT]
 
     total = jnp.sum(dens, axis=1, keepdims=True)
     eye = iota((8, 128), 0) == iota((8, 128), 1)
     part = jnp.sum(jnp.where(eye, total, 0.0), axis=0, keepdims=True)
-    for level in range(3):
-        slot = (xc, z, y)[level]
-        sums[level, slot] = part
-
-        def tell(i, level=level, slot=slot):
-            px, pc = lax.div(i, 2), lax.rem(i, 2)
-            device = (at(px, y, pc, z), at(x, y, c, i), at(x, i, c, z))[level]
-
-            @pl.when(i != slot)
-            def _():
-                push(sums.at[level, slot], sums.at[level, slot], sum_send, sum_sem.at[level], device)
-
-        each(8, tell)
-        settle(sums.at[level, pl.ds(0, 7)], sum_sem.at[level])
-        part = jnp.sum(sums[level, :, 0, :], axis=0, keepdims=True)
+    sums[xc * 8 + z] = part
+
+    def tell(step, some):
+        ring = around(z, step)
+        for px, pc, _ in some:
+            push(sums.at[xc * 8 + z], sums.at[xc * 8 + z], sum_send, sum_sem.at[0], at(px, y, pc, ring))
+
+    def tell_far(i):
+        half = lax.div(i + 1, 2)
+        tell(jnp.where(lax.rem(i, 2) == 0, 4 + half, 4 - half), columns)
+
+    each(7, tell_far)
+    tell(0, columns[:-1])
+    settle(sums.at[pl.ds(0, 63)], sum_sem.at[0])
+    sums2[y] = jnp.sum(sums[:, 0, :], axis=0, keepdims=True)
+    for step in FAR:
+        push(sums2.at[y], sums2.at[y], sum_send, sum_sem.at[1], at(x, around(y, step), c, z))
+    settle(sums2.at[pl.ds(0, 7)], sum_sem.at[1])
+    part = jnp.sum(sums2[:, 0, :], axis=0, keepdims=True)
     magnet[...] = part[:, 0:3] * (1.0 / KPOINTS)
 
-    for level in range(3):
-        settle(sums.at[level, pl.ds(0, 7)], sum_send)
+    settle(sums.at[pl.ds(0, 63)], sum_send)
+    settle(sums2.at[pl.ds(0, 7)], sum_send)
     settle(k_p.at[pl.ds(0, 14)], send1)
     settle(k_p.at[pl.ds(0, 56)], send1)
     settle(k_p.at[pl.ds(0, 56)], send1)
@@ -448,9 +461,12 @@
     density, magnet = pl.pallas_call(
         body,
         out_shape=(jax.ShapeDtypeStruct((3, KPT), F32), jax.ShapeDtypeStruct((1, 3), F32)),
-        in_specs=[vmem, vmem, vmem, anywhere, anywhere],
+        in_specs=[anywhere] * 5,
         out_specs=(vmem, vmem),
         scratch_shapes=[
+            pltpu.VMEM((3, KPT), jnp.int32),
+            pltpu.VMEM((3, NR), jnp.int32),
+            pltpu.VMEM((1, NR), jnp.int32),
             pltpu.VMEM((KPT, 2 * HALF), BF),
             pltpu.VMEM((1, 1, 128), F32),
             pltpu.VMEM((64, 1, 128), F32),
@@ -467,9 +483,10 @@
             pltpu.VMEM((4, CHUNKS, KPT, 2 * CHUNK), BF),
             pltpu.VMEM((8, W * KPT, 128), F32),
             pltpu.VMEM((KPT, 256, 256), BF),
-            pltpu.VMEM((KPT, W, 256), BF),
-            pltpu.VMEM((3, 8, 1, 128), F32),
-            dma, dma, dma, dma((2,)), dma((2,)), dma((2,)), dma((2,)), dma, dma, dma, dma((3,)),
+            pltpu.VMEM((KPT, W, 2 * W), BF),
+            pltpu.VMEM((64, 1, 128), F32),
+            pltpu.VMEM((8, 1, 128), F32),
+            dma, dma, dma, dma((2,)), dma((2,)), dma((2,)), dma((2,)), dma, dma, dma, dma((2,)), dma, dma((2,)),
         ],
         compiler_params=pltpu.CompilerParams(
             collective_id=0, has_side_effects=True, vmem_limit_bytes=56 * 1024 * 1024

time: 66.2 us -> 60.7 us (0.917); the launches traced: 65.3 us -> 60.5 us
  Pallas kernels: 62.8 us -> 58.1 us
    pallas_call x1, Pallas kernels: 62.8 us -> 58.1 us  [per_device(): pl.pallas_call(body, out_shape=(jax.ShapeDtypeStruct((3, KPT), F32), jax....]
where the time goes in v2:
time: 60.7 us; the launch traced here: 60.5 us
  Pallas kernels  58.1 us (96%)
  local copies, waits for them, and re-layouts  1.8 us (3%)
  between operations  0.65 us (1%)
    pallas_call x1, Pallas kernels, per_device(): pl.pallas_call(body, out_shape=(jax.ShapeDtypeStruct((3, KPT), F32), jax....  58.1 us
    unnamed x6, local copies, waits for them, and re-layouts  1.8 us

profile of v2, /device:TPU:1, one launch (start us, length us, event | category | flops | bytes accessed | tf_op | source)
XLA Modules:
  0.0 60.5 jit_solution(16667869359018816761)
XLA Ops:
  0.6 58.1 %orbital.1 = (f32[3,8]{1,0:T(4,128)}, f32[1,3]{1,0:T(1,128)}) custom-call(s32[3,8]{1,0:T(4,128)} %kgrid_hbm.1, s32[3,256]{1,0:T(4,128)} %rvec_hbm.1, s32[1,256]{1,0:T(1,128)} %bitcast.2, bf16[1,2,12800]{2,1,0:T(2,128)(2,1)} %operators.1, bf16[8,12800]{1,0:T(8,128)(2,1)} %vectors.1), custom_call_target="tpu_custom_call" | custom-call | tf_op jit(solution)/shard_map/orbital/pallas_call | solution.py:461
  58.7 0.0 copy-start
  58.7 0.7 %copy-done = f32[3,8]{1,0:T(4,128)S(1)} copy-done((f32[3,8]{1,0:T(4,128)S(1)}, f32[3,8]{1,0:T(4,128)}, u32[]{:S(2)}) %copy-start) | copy-done | bytes 120
  59.4 0.0 copy-start.1
  59.4 0.6 copy.9
  60.0 0.1 copy-done.1
  60.0 0.5 copy.10
Async XLA Ops:
  58.7 0.7 %copy-start = (f32[3,8]{1,0:T(4,128)S(1)}, f32[3,8]{1,0:T(4,128)}, u32[]{:S(2)}) copy-start(f32[3,8]{1,0:T(4,128)} %get-tuple-element.8) | copy-start | bytes 292
  59.4 0.6 %copy-start.1 = (f32[1,3]{1,0:T(1,128)S(1)}, f32[1,3]{1,0:T(1,128)}, u32[]{:S(2)}) copy-start(f32[1,3]{1,0:T(1,128)} %get-tuple-element.5) | copy-start | bytes 40

commit v3 on v2

--- a/solution.py
+++ b/solution.py
@@ -140,10 +140,10 @@
 
 
 def body(
-    kgrid_hbm, rvec_hbm, degen_hbm, operators, vectors, density, magnet,
-    kgrid, rvec, degen, vec, own_row, k_p, k_q, in_p, in_q, stage, all_p, all_q, tab_p, tab_q,
+    kgrid_hbm, rvec_hbm, degen_hbm, operators_hbm, vectors, density, magnet,
+    kgrid, rvec, degen, operators, vec, own_row, k_p, k_q, in_p, in_q, stage, all_p, all_q, tab_p, tab_q,
     out_p, out_q, full, mats, right, left, sums, sums2,
-    send1, send2, send3, k1_sem, k2_sem, in_sem, all_sem, full_sem, vec_sem, sum_send, sum_sem, kg_sem, small_sem,
+    send1, send2, send3, k1_sem, k2_sem, in_sem, all_sem, full_sem, vec_sem, sum_send, sum_sem, kg_sem, small_sem, op_sem,
 ):
     x, y, c, z = place()
     xc = 2 * x + c
@@ -153,17 +153,16 @@
     keep(kgrid_hbm, kgrid, kg_sem)
     keep(rvec_hbm, rvec, small_sem.at[0])
     keep(degen_hbm, degen, small_sem.at[1])
+    keep(operators_hbm, operators, op_sem)
     keep(vectors, vec, vec_sem)
     columns = partners(x, c)
 
-    def greet(step):
-        for px, pc, _ in columns:
-            pl.semaphore_signal(barrier, inc=1, device_id=at(px, y, pc, around(z, step)), device_id_type=MESH)
-            pl.semaphore_signal(barrier, inc=1, device_id=at(px, around(y, step), pc, z), device_id_type=MESH)
-
     for px, pc, _ in columns[:-1]:
         pl.semaphore_signal(barrier, inc=1, device_id=at(px, y, pc, z), device_id_type=MESH)
-    each(7, lambda i: greet(i + 1))
+    for step in FAR:
+        for pc in (c, 1 - c):
+            pl.semaphore_signal(barrier, inc=1, device_id=at(x, y, pc, around(z, step)), device_id_type=MESH)
+            pl.semaphore_signal(barrier, inc=1, device_id=at(x, around(y, step), pc, z), device_id_type=MESH)
     pltpu.make_async_copy(kgrid_hbm, kgrid, kg_sem).wait()
 
     stage[...] = jnp.zeros_like(stage)
@@ -174,7 +173,8 @@
     k_p[xc * 8 + z] = row
     k_q[xc * 8 + y] = row
 
-    pl.semaphore_wait(barrier, 63 + 56)
+    pltpu.make_async_copy(operators_hbm, operators, op_sem).wait()
+    pl.semaphore_wait(barrier, 7 + 14 + 14)
 
     for step in FAR:
         push(own_row.at[0], k_p.at[xc * 8 + z], send1, k1_sem.at[0], at(x, y, c, around(z, step)))
@@ -467,6 +467,7 @@
             pltpu.VMEM((3, KPT), jnp.int32),
             pltpu.VMEM((3, NR), jnp.int32),
             pltpu.VMEM((1, NR), jnp.int32),
+            pltpu.VMEM((1, 2, 2 * HALF), BF),
             pltpu.VMEM((KPT, 2 * HALF), BF),
             pltpu.VMEM((1, 1, 128), F32),
             pltpu.VMEM((64, 1, 128), F32),
@@ -486,7 +487,7 @@
             pltpu.VMEM((KPT, W, 2 * W), BF),
             pltpu.VMEM((64, 1, 128), F32),
             pltpu.VMEM((8, 1, 128), F32),
-            dma, dma, dma, dma((2,)), dma((2,)), dma((2,)), dma((2,)), dma, dma, dma, dma((2,)), dma, dma((2,)),
+            dma, dma, dma, dma((2,)), dma((2,)), dma((2,)), dma((2,)), dma, dma, dma, dma((2,)), dma, dma((2,)), dma,
         ],
         compiler_params=pltpu.CompilerParams(
             collective_id=0, has_side_effects=True, vmem_limit_bytes=56 * 1024 * 1024

time: 60.7 us -> 58.9 us (0.970)
  Pallas kernels: 58.1 us -> 56.3 us
    pallas_call x1, Pallas kernels: 58.1 us -> 56.3 us  [per_device(): pl.pallas_call(body, out_shape=(jax.ShapeDtypeStruct((3, KPT), F32), jax....]
where the time goes in v3:
time: 58.9 us; the launch traced here: 58.8 us
  Pallas kernels  56.3 us (96%)
  local copies, waits for them, and re-layouts  1.8 us (3%)
  between operations  0.65 us (1%)
    pallas_call x1, Pallas kernels, per_device(): pl.pallas_call(body, out_shape=(jax.ShapeDtypeStruct((3, KPT), F32), jax....  56.3 us
    unnamed x6, local copies, waits for them, and re-layouts  1.8 us

profile of v3, /device:TPU:1, one launch (start us, length us, event | category | flops | bytes accessed | tf_op | source)
XLA Modules:
  0.0 58.8 jit_solution(4723201063650696869)
XLA Ops:
  0.6 56.3 %orbital.1 = (f32[3,8]{1,0:T(4,128)}, f32[1,3]{1,0:T(1,128)}) custom-call(s32[3,8]{1,0:T(4,128)} %kgrid_hbm.1, s32[3,256]{1,0:T(4,128)} %rvec_hbm.1, s32[1,256]{1,0:T(1,128)} %bitcast.2, bf16[1,2,12800]{2,1,0:T(2,128)(2,1)} %operators_hbm.1, bf16[8,12800]{1,0:T(8,128)(2,1)} %vectors.1), custom_call_target="tpu_custom_call" | custom-call | tf_op jit(solution)/shard_map/orbital/pallas_call | solution.py:461
  57.0 0.0 copy-start
  57.0 0.7 %copy-done = f32[3,8]{1,0:T(4,128)S(1)} copy-done((f32[3,8]{1,0:T(4,128)S(1)}, f32[3,8]{1,0:T(4,128)}, u32[]{:S(2)}) %copy-start) | copy-done | bytes 120
  57.6 0.0 copy-start.1
  57.6 0.6 copy.9
  58.2 0.1 copy-done.1
  58.3 0.5 copy.10
Async XLA Ops:
  57.0 0.7 %copy-start = (f32[3,8]{1,0:T(4,128)S(1)}, f32[3,8]{1,0:T(4,128)}, u32[]{:S(2)}) copy-start(f32[3,8]{1,0:T(4,128)} %get-tuple-element.8) | copy-start | bytes 292
  57.6 0.6 %copy-start.1 = (f32[1,3]{1,0:T(1,128)S(1)}, f32[1,3]{1,0:T(1,128)}, u32[]{:S(2)}) copy-start(f32[1,3]{1,0:T(1,128)} %get-tuple-element.5) | copy-start | bytes 40

commit v4 on v3

--- a/solution.py
+++ b/solution.py
@@ -21,7 +21,6 @@
 CHUNKS = HALF // CHUNK
 FIRST_Q = 13
 KPOINTS = 4096
-TOGETHER = 2
 MESH = pl.DeviceIdType.MESH
 BF = jnp.bfloat16
 F32 = jnp.float32
@@ -110,14 +109,15 @@
     points = rows_ref[:, 0, :]
     spread = (lax.div(iota((512, 64), 0), 8) == iota((512, 64), 1)).astype(F32).astype(BF)
     wide = dot(spread, points.astype(BF))
-    own = lax.rem(iota((512, 128), 0), 8) == lax.rem(iota((512, 128), 1), 8)
-    wide = jnp.where(own, wide, 0.0).astype(BF)
-    for part in range(4):
-        winding = dot(wide[part * 128:(part + 1) * 128], lattice)
+    shift = (lax.div(lax.rem(iota((128, NR), 0), 8), 4) * (GRID // 4)).astype(F32)
+    for block in range(8):
+        half, rows = block // 4, slice((block % 4) * 128, (block % 4 + 1) * 128)
+        own = half * 4 + lax.rem(iota((128, 128), 0), 4) == lax.rem(iota((128, 128), 1), 8)
+        winding = dot(jnp.where(own, wide[rows], 0.0).astype(BF), lattice) - shift
         winding = winding - GRID * jnp.floor(winding * (1.0 / GRID))
         upper = winding >= GRID // 2
         turn = jnp.where(upper, winding - (GRID // 2), winding) - (GRID // 4)
-        sign = jnp.where(upper, -inverse, inverse)
+        sign = jnp.where(upper, inverse, -inverse)
         angle = turn * (2.0 * math.pi / GRID)
         sq = angle * angle
         odd = -1.0 / 39916800.0
@@ -126,17 +126,16 @@
         even = 1.0 / 479001600.0
         for term in (-1.0 / 3628800.0, 1.0 / 40320.0, -1.0 / 720.0, 1.0 / 24.0, -0.5, 1.0):
             even = even * sq + term
-        table[part * 128:(part + 1) * 128, :NR] = (-odd * angle * sign).astype(BF)
-        table[part * 128:(part + 1) * 128, NR:] = (even * sign).astype(BF)
-
-
-def transform(table, gathered, out):
-    for part in range(4):
-        rows = slice(part * 128, (part + 1) * 128)
+        table[block * 128:(block + 1) * 128, :NR] = (odd * angle * sign).astype(BF)
+        table[block * 128:(block + 1) * 128, NR:] = (even * sign).astype(BF)
+
+
+def transform(table, gathered, out, half):
+    for part in range(2):
+        rows = slice(half * 512 + part * 256, half * 512 + (part + 1) * 256)
         block = gathered[...].reshape(NR, 2 * CHUNK)
-        turned = jnp.concatenate([-block[:, CHUNK:], block[:, :CHUNK]], axis=1)
-        total = dot(table[rows, :NR], block) + dot(table[rows, NR:], turned)
-        out[part * 16:(part + 1) * 16] = total.reshape(16, KPT, 2 * CHUNK).astype(BF)
+        total = dot(table[rows, :NR], block[:, :CHUNK]) + dot(table[rows, NR:], block[:, CHUNK:])
+        out[half, part * 32:(part + 1) * 32] = total.reshape(32, KPT, CHUNK).astype(BF)
 
 
 def body(
@@ -299,14 +298,14 @@
         weights = dot(jnp.broadcast_to(weight, (8, NR)).astype(BF), swap)[0:1]
         fold_table(k_q, moved, 1.0 / weights, tab_q)
 
-    def deliver(chunk, out, along_z):
-        dst = full.at[x, chunk]
+    def deliver(chunk, out, along_z, half):
+        dst = full.at[half, x, chunk]
 
         def one(step, some):
             ring = around(z if along_z else y, step)
             for px, pc, pxc in some:
                 device = at(px, y, pc, ring) if along_z else at(px, ring, pc, z)
-                push(out.at[pxc * 8 + ring], dst, send3, full_sem, device)
+                push(out.at[half, pxc * 8 + ring], dst, send3, full_sem.at[half], device)
 
         def far(i):
             half = lax.div(i + 1, 2)
@@ -314,96 +313,102 @@
 
         each(7, far)
         one(0, columns[:-1])
-        keep(out.at[xc * 8 + (z if along_z else y)], dst, full_sem)
+        keep(out.at[half, xc * 8 + (z if along_z else y)], dst, full_sem.at[half])
 
     @pl.when(live_p)
     def _():
         settle(all_p.at[pl.ds(0, 7)], all_sem.at[0])
-        transform(tab_p, all_p, out_p)
-        deliver(chunk_p, out_p, True)
+        transform(tab_p, all_p, out_p, 0)
+        deliver(chunk_p, out_p, True, 0)
 
     @pl.when(live_q)
     def _():
         settle(all_q.at[pl.ds(0, 7)], all_sem.at[1])
-        transform(tab_q, all_q, out_q)
-        deliver(chunk_q, out_q, False)
-
-    settle(full, full_sem)
-
-    def rebuild(o):
-        for part in range(2):
-            def put(i, val, part=part):
-                mats[2 * o + part, i * KPT:(i + 1) * KPT, :] = val
-
-            matrix_rows(
-                lambda t, part=part: full[o, t // 2, :, part * CHUNK + (t % 2) * 128: part * CHUNK + (t % 2 + 1) * 128].astype(F32),
-                put,
-            )
-
-    each(4, rebuild)
+        transform(tab_q, all_q, out_q, 0)
+        deliver(chunk_q, out_q, False, 0)
+
+    @pl.when(live_p)
+    def _():
+        transform(tab_p, all_p, out_p, 1)
+        deliver(chunk_p, out_p, True, 1)
+
+    @pl.when(live_q)
+    def _():
+        transform(tab_q, all_q, out_q, 1)
+        deliver(chunk_q, out_q, False, 1)
 
     sub = iota((W, 128), 0)
-    density_lane = iota((1, 128), 1)
-
-    def point(k, carry):
-        ops = [
-            jnp.concatenate(
-                [mats[2 * o, pl.ds(k, W, stride=KPT), :], mats[2 * o + 1, pl.ds(k, W, stride=KPT), :]], axis=1
-            ).astype(BF)
-            for o in range(4)
-        ]
-        prod = dot(jnp.concatenate(ops, axis=0), right[k])
-        turn = left[k]
-        rot = []
+
+    def rotate(half):
+        settle(full.at[half], full_sem.at[half])
+
+        def rebuild(o):
+            def put(i, val):
+                mats[o, i * KPT:(i + 1) * KPT, :] = val
+
+            matrix_rows(lambda t: full[half, o, t // 2, :, (t % 2) * 128:(t % 2 + 1) * 128].astype(F32), put)
+
+        each(4, rebuild)
+        group = range(4)
+        prods = []
+        for k in group:
+            ops = [
+                jnp.concatenate(
+                    [mats[o, pl.ds(k, W, stride=KPT), :], mats[o, pl.ds(4 + k, W, stride=KPT), :]], axis=1
+                ).astype(BF)
+                for o in range(4)
+            ]
+            prods.append(dot(jnp.concatenate(ops, axis=0), right[half * 4 + k]).astype(BF))
+        rots = [[] for _ in group]
         for o in range(4):
-            re = prod[o * W:(o + 1) * W, :128]
-            im = prod[o * W:(o + 1) * W, 128:]
-            stacked = jnp.concatenate(
-                [jnp.concatenate([re, im], axis=1), jnp.concatenate([im, -re], axis=1)],
-                axis=0,
-            ).astype(BF)
-            rot.append(dot(turn, stacked).astype(BF).astype(F32))
-        ham_re, ham_im = rot[0][:, :128], rot[0][:, 128:]
-        diag = jnp.where(sub == lane, ham_re, 0.0)
-        down = 1.0 / (1.0 + jnp.exp(jnp.sum(diag, axis=1, keepdims=True) * (1.0 / SMEARING)))
-        along = 1.0 / (1.0 + jnp.exp(jnp.sum(diag, axis=0, keepdims=True) * (1.0 / SMEARING)))
-        weight2 = (1.0 - down) * along
-        ham = paired(ham_re, ham_im).astype(BF)
-        prods, turned = [], []
+            for k in group:
+                re = prods[k][o * W:(o + 1) * W, :128]
+                im = prods[k][o * W:(o + 1) * W, 128:]
+                stacked = jnp.concatenate(
+                    [jnp.concatenate([re, im], axis=1), jnp.concatenate([im, -re], axis=1)], axis=0
+                )
+                rots[k].append(dot(left[half * 4 + k], stacked).astype(BF))
+        hams, weights = [], []
+        for k in group:
+            ham_re, ham_im = rots[k][0][:, :128].astype(F32), rots[k][0][:, 128:].astype(F32)
+            diag = jnp.where(sub == lane, ham_re, 0.0)
+            down = 1.0 / (1.0 + jnp.exp(jnp.sum(diag, axis=1, keepdims=True) * (1.0 / SMEARING)))
+            along = 1.0 / (1.0 + jnp.exp(jnp.sum(diag, axis=0, keepdims=True) * (1.0 / SMEARING)))
+            weights.append((1.0 - down) * along)
+            hams.append(paired(ham_re, ham_im).astype(BF))
+        products = [[] for _ in group]
+        turned = [[] for _ in group]
         fill = jnp.zeros((48, 128), F32)
         for b in range(3):
-            re, im = rot[b + 1][:, :128], rot[b + 1][:, 128:]
-            stacked = jnp.concatenate(
-                [jnp.concatenate([re, im], axis=1), jnp.concatenate([-im, re], axis=1)],
-                axis=0,
-            ).astype(BF)
-            prods.append(dot(ham, stacked))
-            turned.append((
-                jnp.transpose(jnp.concatenate([re, fill], axis=0))[:W] * weight2,
-                jnp.transpose(jnp.concatenate([im, fill], axis=0))[:W] * weight2,
-            ))
+            for k in group:
+                re, im = rots[k][b + 1][:, :128], rots[k][b + 1][:, 128:]
+                stacked = jnp.concatenate(
+                    [jnp.concatenate([re, im], axis=1), jnp.concatenate([-im, re], axis=1)], axis=0
+                )
+                products[k].append(dot(hams[k], stacked))
+                turned[k].append((
+                    jnp.transpose(jnp.concatenate([re.astype(F32), fill], axis=0))[:W],
+                    jnp.transpose(jnp.concatenate([im.astype(F32), fill], axis=0))[:W],
+                ))
+        spot8 = iota((KPT, 128), 0)
         for comp, (a, b) in enumerate(((1, 2), (2, 0), (0, 1))):
-            terms = (
-                turned[a][0] * prods[b][:, 128:] + turned[a][1] * prods[b][:, :128]
-                - turned[b][0] * prods[a][:, 128:] - turned[b][1] * prods[a][:, :128]
-            )
-            total = jnp.sum(jnp.sum(terms, axis=0, keepdims=True), axis=1, keepdims=True) * (1.0 / W)
-            stage[comp:comp + 1, 0:128] = stage[comp:comp + 1, 0:128] + jnp.where(density_lane == k, total, 0.0)
-        return carry
-
-    stage[0:8, 0:128] = jnp.zeros((8, 128), F32)
-    def points(i, carry):
-        for j in range(TOGETHER):
-            carry = point(TOGETHER * i + j, carry)
-        return carry
-
-    lax.fori_loop(0, KPT // TOGETHER, points, 0)
-    dens = stage[0:8, 0:128]
-    density[...] = dens[0:3, 0:KPT]
-
-    total = jnp.sum(dens, axis=1, keepdims=True)
-    eye = iota((8, 128), 0) == iota((8, 128), 1)
-    part = jnp.sum(jnp.where(eye, total, 0.0), axis=0, keepdims=True)
+            found = jnp.zeros((KPT, 128), F32)
+            for k in group:
+                terms = (
+                    turned[k][a][0] * products[k][b][:, 128:] + turned[k][a][1] * products[k][b][:, :128]
+                    - turned[k][b][0] * products[k][a][:, 128:] - turned[k][b][1] * products[k][a][:, :128]
+                ) * weights[k]
+                found = jnp.where(spot8 == half * 4 + k, jnp.sum(terms, axis=0, keepdims=True) * (1.0 / W), found)
+            stage[comp * KPT:(comp + 1) * KPT, 0:128] = stage[comp * KPT:(comp + 1) * KPT, 0:128] + found
+
+    stage[...] = jnp.zeros_like(stage)
+    each(2, rotate)
+    spot = iota((1, 128), 1)
+    part = jnp.zeros((1, 128), F32)
+    for comp in range(3):
+        sumk = jnp.sum(stage[comp * KPT:(comp + 1) * KPT, 0:128], axis=0, keepdims=True)
+        part = part + jnp.where(spot == comp, jnp.sum(sumk, axis=1, keepdims=True), 0.0)
+
     sums[xc * 8 + z] = part
 
     def tell(step, some):
@@ -417,6 +422,10 @@
 
     each(7, tell_far)
     tell(0, columns[:-1])
+    eye = iota((KPT, 128), 0) == iota((KPT, 128), 1)
+    for comp in range(3):
+        column = jnp.sum(stage[comp * KPT:(comp + 1) * KPT, 0:128], axis=1, keepdims=True)
+        density[comp:comp + 1] = jnp.sum(jnp.where(eye, column, 0.0), axis=0, keepdims=True)[:, 0:KPT]
     settle(sums.at[pl.ds(0, 63)], sum_sem.at[0])
     sums2[y] = jnp.sum(sums[:, 0, :], axis=0, keepdims=True)
     for step in FAR:
@@ -446,12 +455,14 @@
     @pl.when(live_p)
     def _():
         settle(all_p.at[pl.ds(0, 7)], send3)
-        settle(out_p.at[pl.ds(0, 63)], send3)
+        for half in range(2):
+            settle(out_p.at[half, pl.ds(0, 63)], send3)
 
     @pl.when(live_q)
     def _():
         settle(all_q.at[pl.ds(0, 7)], send3)
-        settle(out_q.at[pl.ds(0, 63)], send3)
+        for half in range(2):
+            settle(out_q.at[half, pl.ds(0, 63)], send3)
 
 
 def per_device(kgrid, rvec, degen, operators, vectors):
@@ -477,17 +488,17 @@
             pltpu.VMEM((32, 2 * CHUNK), F32),
             pltpu.VMEM((RING, 32, 2 * CHUNK), BF),
             pltpu.VMEM((RING, 32, 2 * CHUNK), BF),
-            pltpu.VMEM((512, 2 * NR), BF),
-            pltpu.VMEM((512, 2 * NR), BF),
-            pltpu.VMEM((64, KPT, 2 * CHUNK), BF),
-            pltpu.VMEM((64, KPT, 2 * CHUNK), BF),
-            pltpu.VMEM((4, CHUNKS, KPT, 2 * CHUNK), BF),
-            pltpu.VMEM((8, W * KPT, 128), F32),
+            pltpu.VMEM((1024, 2 * NR), BF),
+            pltpu.VMEM((1024, 2 * NR), BF),
+            pltpu.VMEM((2, 64, KPT, CHUNK), BF),
+            pltpu.VMEM((2, 64, KPT, CHUNK), BF),
+            pltpu.VMEM((2, 4, CHUNKS, KPT, CHUNK), BF),
+            pltpu.VMEM((4, W * KPT, 128), F32),
             pltpu.VMEM((KPT, 256, 256), BF),
             pltpu.VMEM((KPT, W, 2 * W), BF),
             pltpu.VMEM((64, 1, 128), F32),
             pltpu.VMEM((8, 1, 128), F32),
-            dma, dma, dma, dma((2,)), dma((2,)), dma((2,)), dma((2,)), dma, dma, dma, dma((2,)), dma, dma((2,)), dma,
+            dma, dma, dma, dma((2,)), dma((2,)), dma((2,)), dma((2,)), dma((2,)), dma, dma, dma((2,)), dma, dma((2,)), dma,
         ],
         compiler_params=pltpu.CompilerParams(
             collective_id=0, has_side_effects=True, vmem_limit_bytes=56 * 1024 * 1024

time: 58.9 us -> 55.5 us (0.942)
  Pallas kernels: 56.3 us -> 52.8 us
    pallas_call x1, Pallas kernels: 56.3 us -> 52.8 us  [per_device(): pl.pallas_call(body, out_shape=(jax.ShapeDtypeStruct((3, KPT), F32), jax....]
where the time goes in v4:
time: 55.5 us; the launch traced here: 55.3 us
  Pallas kernels  52.8 us (95%)
  local copies, waits for them, and re-layouts  1.8 us (3%)
  between operations  0.65 us (1%)
    pallas_call x1, Pallas kernels, per_device(): pl.pallas_call(body, out_shape=(jax.ShapeDtypeStruct((3, KPT), F32), jax....  52.8 us
    unnamed x6, local copies, waits for them, and re-layouts  1.8 us

profile of v4, /device:TPU:1, one launch (start us, length us, event | category | flops | bytes accessed | tf_op | source)
XLA Modules:
  0.0 55.3 jit_solution(7078540208839721588)
XLA Ops:
  0.6 52.8 %orbital.1 = (f32[3,8]{1,0:T(4,128)}, f32[1,3]{1,0:T(1,128)}) custom-call(s32[3,8]{1,0:T(4,128)} %kgrid_hbm.1, s32[3,256]{1,0:T(4,128)} %rvec_hbm.1, s32[1,256]{1,0:T(1,128)} %bitcast.2, bf16[1,2,12800]{2,1,0:T(2,128)(2,1)} %operators_hbm.1, bf16[8,12800]{1,0:T(8,128)(2,1)} %vectors.1), custom_call_target="tpu_custom_call" | custom-call | tf_op jit(solution)/shard_map/orbital/pallas_call | solution.py:472
  53.5 0.0 copy-start
  53.5 0.7 %copy-done = f32[3,8]{1,0:T(4,128)S(1)} copy-done((f32[3,8]{1,0:T(4,128)S(1)}, f32[3,8]{1,0:T(4,128)}, u32[]{:S(2)}) %copy-start) | copy-done | bytes 120
  54.1 0.0 copy-start.1
  54.1 0.6 %copy.9 = f32[3,8]{1,0:T(4,128)} copy(f32[3,8]{1,0:T(4,128)S(1)} %copy-done) | data formatting | bytes 192
  54.7 0.1 copy-done.1
  54.8 0.5 copy.10
Async XLA Ops:
  53.5 0.7 %copy-start = (f32[3,8]{1,0:T(4,128)S(1)}, f32[3,8]{1,0:T(4,128)}, u32[]{:S(2)}) copy-start(f32[3,8]{1,0:T(4,128)} %get-tuple-element.8) | copy-start | bytes 292
  54.1 0.6 %copy-start.1 = (f32[1,3]{1,0:T(1,128)S(1)}, f32[1,3]{1,0:T(1,128)}, u32[]{:S(2)}) copy-start(f32[1,3]{1,0:T(1,128)} %get-tuple-element.5) | copy-start | bytes 40

commit v5 on v4

--- a/solution.py
+++ b/solution.py
@@ -107,13 +107,13 @@
 
 def fold_table(rows_ref, lattice, inverse, table):
     points = rows_ref[:, 0, :]
-    spread = (lax.div(iota((512, 64), 0), 8) == iota((512, 64), 1)).astype(F32).astype(BF)
+    spread = (lax.div(iota((256, 64), 0), 4) == iota((256, 64), 1)).astype(F32).astype(BF)
     wide = dot(spread, points.astype(BF))
-    shift = (lax.div(lax.rem(iota((128, NR), 0), 8), 4) * (GRID // 4)).astype(F32)
-    for block in range(8):
-        half, rows = block // 4, slice((block % 4) * 128, (block % 4 + 1) * 128)
+    first = lax.rem(iota((128, NR), 0), 8) < 4
+    for block in range(4):
+        half, rows = block // 2, slice((block % 2) * 128, (block % 2 + 1) * 128)
         own = half * 4 + lax.rem(iota((128, 128), 0), 4) == lax.rem(iota((128, 128), 1), 8)
-        winding = dot(jnp.where(own, wide[rows], 0.0).astype(BF), lattice) - shift
+        winding = dot(jnp.where(own, wide[rows], 0.0).astype(BF), lattice)
         winding = winding - GRID * jnp.floor(winding * (1.0 / GRID))
         upper = winding >= GRID // 2
         turn = jnp.where(upper, winding - (GRID // 2), winding) - (GRID // 4)
@@ -126,8 +126,21 @@
         even = 1.0 / 479001600.0
         for term in (-1.0 / 3628800.0, 1.0 / 40320.0, -1.0 / 720.0, 1.0 / 24.0, -0.5, 1.0):
             even = even * sq + term
-        table[block * 128:(block + 1) * 128, :NR] = (odd * angle * sign).astype(BF)
-        table[block * 128:(block + 1) * 128, NR:] = (even * sign).astype(BF)
+        cosine = odd * angle * sign
+        minus = even * sign
+        pairs = []
+        for upper_part, lower_part in ((cosine, -minus), (minus, cosine)):
+            swapped_low = swap4(lower_part)
+            swapped_up = swap4(upper_part)
+            even_slot = jnp.where(first, upper_part, swapped_low).reshape(16, 1, 8, NR)
+            odd_slot = jnp.where(first, swapped_up, lower_part).reshape(16, 1, 8, NR)
+            pairs.append(jnp.concatenate([even_slot, odd_slot], axis=1).reshape(256, NR))
+        table[block * 256:(block + 1) * 256, :NR] = pairs[0].astype(BF)
+        table[block * 256:(block + 1) * 256, NR:] = pairs[1].astype(BF)
+
+
+def swap4(val):
+    return pltpu.roll(val.reshape(16, 8, NR), 4, 1).reshape(128, NR)
 
 
 def transform(table, gathered, out, half):
@@ -242,14 +255,81 @@
     def _():
         collect(in_q, all_q, z, in_sem.at[1], all_sem.at[1], False)
 
+    lane = iota((W, 128), 1)
+
+    pltpu.make_async_copy(rvec_hbm, rvec, small_sem.at[0]).wait()
+    pltpu.make_async_copy(degen_hbm, degen, small_sem.at[1]).wait()
+    settle(k_p.at[pl.ds(0, 56)], k2_sem.at[0])
+    settle(k_q.at[pl.ds(0, 56)], k2_sem.at[1])
+    lattice_rows = iota((128, NR), 0)
+    rv = rvec[...].astype(F32)
+    lattice = jnp.where(
+        lattice_rows < 8, rv[0:1],
+        jnp.where(lattice_rows < 16, rv[1:2], jnp.where(lattice_rows < 24, rv[2:3], 0.0)),
+    )
+    weight = degen[...].astype(F32)
+
+    @pl.when(live_p)
+    def _():
+        fold_table(k_p, lattice.astype(BF), 1.0 / weight, tab_p)
+
+    @pl.when(live_q)
+    def _():
+        col = iota((NR, NR), 1)
+        source = (
+            lax.rem(lax.div(col, 2), 8) * 32 + lax.rem(lax.div(col, 16), 2) * 16
+            + lax.div(col, 32) * 2 + lax.rem(col, 2)
+        )
+        swap = (iota((NR, NR), 0) == source).astype(F32).astype(BF)
+        moved = dot(lattice.astype(BF), swap).astype(BF)
+        weights = dot(jnp.broadcast_to(weight, (8, NR)).astype(BF), swap)[0:1]
+        fold_table(k_q, moved, 1.0 / weights, tab_q)
+
+    def deliver(chunk, out, along_z, half):
+        dst = full.at[half, x, chunk]
+
+        def one(step, some):
+            ring = around(z if along_z else y, step)
+            for px, pc, pxc in some:
+                device = at(px, y, pc, ring) if along_z else at(px, ring, pc, z)
+                push(out.at[half, pxc * 8 + ring], dst, send3, full_sem.at[half], device)
+
+        def far(i):
+            half = lax.div(i + 1, 2)
+            one(jnp.where(lax.rem(i, 2) == 0, 4 + half, 4 - half), columns)
+
+        each(7, far)
+        one(0, columns[:-1])
+        keep(out.at[half, xc * 8 + (z if along_z else y)], dst, full_sem.at[half])
+
+    @pl.when(live_p)
+    def _():
+        settle(all_p.at[pl.ds(0, 7)], all_sem.at[0])
+        transform(tab_p, all_p, out_p, 0)
+        deliver(chunk_p, out_p, True, 0)
+
+    @pl.when(live_q)
+    def _():
+        settle(all_q.at[pl.ds(0, 7)], all_sem.at[1])
+        transform(tab_q, all_q, out_q, 0)
+        deliver(chunk_q, out_q, False, 0)
+
+    @pl.when(live_p)
+    def _():
+        transform(tab_p, all_p, out_p, 1)
+        deliver(chunk_p, out_p, True, 1)
+
+    @pl.when(live_q)
+    def _():
+        transform(tab_q, all_q, out_q, 1)
+        deliver(chunk_q, out_q, False, 1)
+
     pltpu.make_async_copy(vectors, vec, vec_sem).wait()
     for part in range(2):
         def put(i, val, part=part):
             mats[part, i * KPT:(i + 1) * KPT, :] = val
 
         matrix_rows(lambda t, part=part: vec[:, part * HALF + t * 128: part * HALF + (t + 1) * 128].astype(F32), put)
-
-    lane = iota((W, 128), 1)
 
     def eigen(k):
         vr = mats[0, pl.ds(k, W, stride=KPT), :]
@@ -269,73 +349,6 @@
         return jnp.concatenate([jnp.where(lane < W, re, moved), moved[:, :2 * W - 128]], axis=1)
 
     each(KPT, eigen)
-
-    pltpu.make_async_copy(rvec_hbm, rvec, small_sem.at[0]).wait()
-    pltpu.make_async_copy(degen_hbm, degen, small_sem.at[1]).wait()
-    settle(k_p.at[pl.ds(0, 56)], k2_sem.at[0])
-    settle(k_q.at[pl.ds(0, 56)], k2_sem.at[1])
-    lattice_rows = iota((128, NR), 0)
-    rv = rvec[...].astype(F32)
-    lattice = jnp.where(
-        lattice_rows < 8, rv[0:1],
-        jnp.where(lattice_rows < 16, rv[1:2], jnp.where(lattice_rows < 24, rv[2:3], 0.0)),
-    )
-    weight = degen[...].astype(F32)
-
-    @pl.when(live_p)
-    def _():
-        fold_table(k_p, lattice.astype(BF), 1.0 / weight, tab_p)
-
-    @pl.when(live_q)
-    def _():
-        col = iota((NR, NR), 1)
-        source = (
-            lax.rem(lax.div(col, 2), 8) * 32 + lax.rem(lax.div(col, 16), 2) * 16
-            + lax.div(col, 32) * 2 + lax.rem(col, 2)
-        )
-        swap = (iota((NR, NR), 0) == source).astype(F32).astype(BF)
-        moved = dot(lattice.astype(BF), swap).astype(BF)
-        weights = dot(jnp.broadcast_to(weight, (8, NR)).astype(BF), swap)[0:1]
-        fold_table(k_q, moved, 1.0 / weights, tab_q)
-
-    def deliver(chunk, out, along_z, half):
-        dst = full.at[half, x, chunk]
-
-        def one(step, some):
-            ring = around(z if along_z else y, step)
-            for px, pc, pxc in some:
-                device = at(px, y, pc, ring) if along_z else at(px, ring, pc, z)
-                push(out.at[half, pxc * 8 + ring], dst, send3, full_sem.at[half], device)
-
-        def far(i):
-            half = lax.div(i + 1, 2)
-            one(jnp.where(lax.rem(i, 2) == 0, 4 + half, 4 - half), columns)
-
-        each(7, far)
-        one(0, columns[:-1])
-        keep(out.at[half, xc * 8 + (z if along_z else y)], dst, full_sem.at[half])
-
-    @pl.when(live_p)
-    def _():
-        settle(all_p.at[pl.ds(0, 7)], all_sem.at[0])
-        transform(tab_p, all_p, out_p, 0)
-        deliver(chunk_p, out_p, True, 0)
-
-    @pl.when(live_q)
-    def _():
-        settle(all_q.at[pl.ds(0, 7)], all_sem.at[1])
-        transform(tab_q, all_q, out_q, 0)
-        deliver(chunk_q, out_q, False, 0)
-
-    @pl.when(live_p)
-    def _():
-        transform(tab_p, all_p, out_p, 1)
-        deliver(chunk_p, out_p, True, 1)
-
-    @pl.when(live_q)
-    def _():
-        transform(tab_q, all_q, out_q, 1)
-        deliver(chunk_q, out_q, False, 1)
 
     sub = iota((W, 128), 0)
 
@@ -471,7 +484,7 @@
     dma = pltpu.SemaphoreType.DMA
     density, magnet = pl.pallas_call(
         body,
-        out_shape=(jax.ShapeDtypeStruct((3, KPT), F32), jax.ShapeDtypeStruct((1, 3), F32)),
+        out_shape=(pltpu.VMEM((3, KPT), F32), pltpu.VMEM((1, 3), F32)),
         in_specs=[anywhere] * 5,
         out_specs=(vmem, vmem),
         scratch_shapes=[

time: 55.5 us -> 54.1 us (0.975)
  local copies, waits for them, and re-layouts: 1.8 us -> 1.09 us
    unnamed x6 -> x2, local copies, waits for them, and re-layouts: 1.8 us -> 1.09 us
    pallas_call x1, Pallas kernels: 52.8 us -> 52.3 us  [per_device(): pl.pallas_call(body, out_shape=(pltpu.VMEM((3, KPT), F32), pltpu.VMEM((1,...]
where the time goes in v5:
time: 54.1 us; the launch traced here: 54 us
  Pallas kernels  52.3 us (97%)
  local copies, waits for them, and re-layouts  1.09 us (2%)
  between operations  0.64 us (1%)
    pallas_call x1, Pallas kernels, per_device(): pl.pallas_call(body, out_shape=(pltpu.VMEM((3, KPT), F32), pltpu.VMEM((1,...  52.3 us
    unnamed x2, local copies, waits for them, and re-layouts  1.09 us

profile of v5, /device:TPU:1, one launch (start us, length us, event | category | flops | bytes accessed | tf_op | source)
XLA Modules:
  0.0 54.0 jit_solution(11714247481254383265)
XLA Ops:
  0.6 52.3 %orbital.1 = (f32[3,8]{1,0:T(4,128)S(1)}, f32[1,3]{1,0:T(1,128)S(1)}) custom-call(s32[3,8]{1,0:T(4,128)} %kgrid_hbm.1, s32[3,256]{1,0:T(4,128)} %rvec_hbm.1, s32[1,256]{1,0:T(1,128)} %bitcast.3, bf16[1,2,12800]{2,1,0:T(2,128)(2,1)} %operators_hbm.1, bf16[8,12800]{1,0:T(8,128)(2,1)} %vectors.1), custom_call_target="tpu_custom_call" | custom-call | tf_op jit(solution)/shard_map/orbital/pallas_call | solution.py:485
  52.9 0.6 %copy.9 = f32[3,8]{1,0:T(4,128)} copy(f32[3,8]{1,0:T(4,128)S(1)} %get-tuple-element.6) | data formatting | bytes 192
  53.5 0.5 copy.10

commit v6 on v5

--- a/solution.py
+++ b/solution.py
@@ -143,19 +143,19 @@
     return pltpu.roll(val.reshape(16, 8, NR), 4, 1).reshape(128, NR)
 
 
-def transform(table, gathered, out, half):
+def transform(table, gathered, out, side, half):
     for part in range(2):
         rows = slice(half * 512 + part * 256, half * 512 + (part + 1) * 256)
-        block = gathered[...].reshape(NR, 2 * CHUNK)
-        total = dot(table[rows, :NR], block[:, :CHUNK]) + dot(table[rows, NR:], block[:, CHUNK:])
-        out[half, part * 32:(part + 1) * 32] = total.reshape(32, KPT, CHUNK).astype(BF)
+        block = gathered[side].reshape(NR, 2 * 128)
+        total = dot(table[rows, :NR], block[:, :128]) + dot(table[rows, NR:], block[:, 128:])
+        out[half, side, part * 32:(part + 1) * 32] = total.reshape(32, KPT, 128).astype(BF)
 
 
 def body(
-    kgrid_hbm, rvec_hbm, degen_hbm, operators_hbm, vectors, density, magnet,
+    kgrid_hbm, rvec_hbm, degen_hbm, operators_hbm, vectors, result,
     kgrid, rvec, degen, operators, vec, own_row, k_p, k_q, in_p, in_q, stage, all_p, all_q, tab_p, tab_q,
     out_p, out_q, full, mats, right, left, sums, sums2,
-    send1, send2, send3, k1_sem, k2_sem, in_sem, all_sem, full_sem, vec_sem, sum_send, sum_sem, kg_sem, small_sem, op_sem,
+    send1, send2, send3, k1_sem, k2_sem, in_sem, p_sem, q_sem, full_sem, vec_sem, sum_send, sum_sem, kg_sem, small_sem, op_sem,
 ):
     x, y, c, z = place()
     xc = 2 * x + c
@@ -188,10 +188,6 @@
     pltpu.make_async_copy(operators_hbm, operators, op_sem).wait()
     pl.semaphore_wait(barrier, 7 + 14 + 14)
 
-    for step in FAR:
-        push(own_row.at[0], k_p.at[xc * 8 + z], send1, k1_sem.at[0], at(x, y, c, around(z, step)))
-        push(own_row.at[0], k_q.at[xc * 8 + y], send1, k1_sem.at[1], at(x, around(y, step), c, z))
-
     def pieces(chunk, dst, sem, device, local):
         for part in range(2):
             col = pl.multiple_of(part * HALF + chunk * CHUNK, 128)
@@ -229,6 +225,10 @@
     def _():
         pieces(chunk_q, in_q.at[c * 8 + y], in_sem.at[1], None, True)
 
+    for step in FAR:
+        push(own_row.at[0], k_p.at[xc * 8 + z], send1, k1_sem.at[0], at(x, y, c, around(z, step)))
+        push(own_row.at[0], k_q.at[xc * 8 + y], send1, k1_sem.at[1], at(x, around(y, step), c, z))
+
     settle(k_p.at[pl.ds(0, 7)], k1_sem.at[0])
     settle(k_q.at[pl.ds(0, 7)], k1_sem.at[1])
 
@@ -241,19 +241,22 @@
         for s in range(16):
             for part in range(2):
                 stage[2 * s:2 * s + 2, part * CHUNK:(part + 1) * CHUNK] = incoming[s, part].astype(F32)
-        gathered[slot] = stage[...].astype(BF)
-
-        for step in FAR:
-            device = at(x, around(y, step), c, z) if along_y else at(x, y, c, around(z, step))
-            push(gathered.at[slot], gathered.at[slot], send3, gather_sem, device)
+        for side in range(2):
+            own = slice(side * 128, side * 128 + 128), slice(CHUNK + side * 128, CHUNK + side * 128 + 128)
+            gathered[side, slot] = jnp.concatenate([stage[:, own[0]], stage[:, own[1]]], axis=1).astype(BF)
+
+        for side in range(2):
+            for step in FAR:
+                device = at(x, around(y, step), c, z) if along_y else at(x, y, c, around(z, step))
+                push(gathered.at[side, slot], gathered.at[side, slot], send3, gather_sem.at[side], device)
 
     @pl.when(live_p)
     def _():
-        collect(in_p, all_p, y, in_sem.at[0], all_sem.at[0], True)
+        collect(in_p, all_p, y, in_sem.at[0], p_sem, True)
 
     @pl.when(live_q)
     def _():
-        collect(in_q, all_q, z, in_sem.at[1], all_sem.at[1], False)
+        collect(in_q, all_q, z, in_sem.at[1], q_sem, False)
 
     lane = iota((W, 128), 1)
 
@@ -285,44 +288,41 @@
         weights = dot(jnp.broadcast_to(weight, (8, NR)).astype(BF), swap)[0:1]
         fold_table(k_q, moved, 1.0 / weights, tab_q)
 
-    def deliver(chunk, out, along_z, half):
-        dst = full.at[half, x, chunk]
+    def deliver(chunk, out, along_z, side, half):
+        dst = full.at[half, x, chunk, side]
+        sem = full_sem.at[half]
 
         def one(step, some):
             ring = around(z if along_z else y, step)
             for px, pc, pxc in some:
                 device = at(px, y, pc, ring) if along_z else at(px, ring, pc, z)
-                push(out.at[half, pxc * 8 + ring], dst, send3, full_sem.at[half], device)
-
-        def far(i):
-            half = lax.div(i + 1, 2)
-            one(jnp.where(lax.rem(i, 2) == 0, 4 + half, 4 - half), columns)
-
-        each(7, far)
+                push(out.at[half, side, pxc * 8 + ring], dst, send3, sem, device)
+
+        for step in FAR:
+            one(step, columns)
         one(0, columns[:-1])
-        keep(out.at[half, xc * 8 + (z if along_z else y)], dst, full_sem.at[half])
-
-    @pl.when(live_p)
-    def _():
-        settle(all_p.at[pl.ds(0, 7)], all_sem.at[0])
-        transform(tab_p, all_p, out_p, 0)
-        deliver(chunk_p, out_p, True, 0)
-
-    @pl.when(live_q)
-    def _():
-        settle(all_q.at[pl.ds(0, 7)], all_sem.at[1])
-        transform(tab_q, all_q, out_q, 0)
-        deliver(chunk_q, out_q, False, 0)
-
-    @pl.when(live_p)
-    def _():
-        transform(tab_p, all_p, out_p, 1)
-        deliver(chunk_p, out_p, True, 1)
-
-    @pl.when(live_q)
-    def _():
-        transform(tab_q, all_q, out_q, 1)
-        deliver(chunk_q, out_q, False, 1)
+        keep(out.at[half, side, xc * 8 + (z if along_z else y)], dst, sem)
+
+    def serve_p(side, half):
+        @pl.when(live_p)
+        def _():
+            if half == 0:
+                settle(all_p.at[side, pl.ds(0, 7)], p_sem.at[side])
+            transform(tab_p, all_p, out_p, side, half)
+            deliver(chunk_p, out_p, True, side, half)
+
+    def serve_q(side, half):
+        @pl.when(live_q)
+        def _():
+            if half == 0:
+                settle(all_q.at[side, pl.ds(0, 7)], q_sem.at[side])
+            transform(tab_q, all_q, out_q, side, half)
+            deliver(chunk_q, out_q, False, side, half)
+
+    for side in range(2):
+        for half in range(2):
+            serve_p(side, half)
+            serve_q(side, half)
 
     pltpu.make_async_copy(vectors, vec, vec_sem).wait()
     for part in range(2):
@@ -359,7 +359,7 @@
             def put(i, val):
                 mats[o, i * KPT:(i + 1) * KPT, :] = val
 
-            matrix_rows(lambda t: full[half, o, t // 2, :, (t % 2) * 128:(t % 2 + 1) * 128].astype(F32), put)
+            matrix_rows(lambda t: full[half, o, t // 2, t % 2].astype(F32), put)
 
         each(4, rebuild)
         group = range(4)
@@ -438,14 +438,14 @@
     eye = iota((KPT, 128), 0) == iota((KPT, 128), 1)
     for comp in range(3):
         column = jnp.sum(stage[comp * KPT:(comp + 1) * KPT, 0:128], axis=1, keepdims=True)
-        density[comp:comp + 1] = jnp.sum(jnp.where(eye, column, 0.0), axis=0, keepdims=True)[:, 0:KPT]
+        result[comp:comp + 1] = jnp.sum(jnp.where(eye, column, 0.0), axis=0, keepdims=True)
     settle(sums.at[pl.ds(0, 63)], sum_sem.at[0])
     sums2[y] = jnp.sum(sums[:, 0, :], axis=0, keepdims=True)
     for step in FAR:
         push(sums2.at[y], sums2.at[y], sum_send, sum_sem.at[1], at(x, around(y, step), c, z))
     settle(sums2.at[pl.ds(0, 7)], sum_sem.at[1])
     part = jnp.sum(sums2[:, 0, :], axis=0, keepdims=True)
-    magnet[...] = part[:, 0:3] * (1.0 / KPOINTS)
+    result[3:4] = part * (1.0 / KPOINTS)
 
     settle(sums.at[pl.ds(0, 63)], sum_send)
     settle(sums2.at[pl.ds(0, 7)], sum_send)
@@ -467,26 +467,30 @@
 
     @pl.when(live_p)
     def _():
-        settle(all_p.at[pl.ds(0, 7)], send3)
+        for side in range(2):
+            settle(all_p.at[side, pl.ds(0, 7)], send3)
         for half in range(2):
-            settle(out_p.at[half, pl.ds(0, 63)], send3)
+            for side in range(2):
+                settle(out_p.at[half, side, pl.ds(0, 63)], send3)
 
     @pl.when(live_q)
     def _():
-        settle(all_q.at[pl.ds(0, 7)], send3)
+        for side in range(2):
+            settle(all_q.at[side, pl.ds(0, 7)], send3)
         for half in range(2):
-            settle(out_q.at[half, pl.ds(0, 63)], send3)
+            for side in range(2):
+                settle(out_q.at[half, side, pl.ds(0, 63)], send3)
 
 
 def per_device(kgrid, rvec, degen, operators, vectors):
     vmem = pl.BlockSpec(memory_space=pltpu.VMEM)
     anywhere = pl.BlockSpec(memory_space=pl.ANY)
     dma = pltpu.SemaphoreType.DMA
-    density, magnet = pl.pallas_call(
+    result = pl.pallas_call(
         body,
-        out_shape=(pltpu.VMEM((3, KPT), F32), pltpu.VMEM((1, 3), F32)),
+        out_shape=pltpu.VMEM((8, 128), F32),
         in_specs=[anywhere] * 5,
-        out_specs=(vmem, vmem),
+        out_specs=vmem,
         scratch_shapes=[
             pltpu.VMEM((3, KPT), jnp.int32),
             pltpu.VMEM((3, NR), jnp.int32),
@@ -499,26 +503,26 @@
             pltpu.VMEM((16, 2, 2, CHUNK), BF),
             pltpu.VMEM((16, 2, 2, CHUNK), BF),
             pltpu.VMEM((32, 2 * CHUNK), F32),
-            pltpu.VMEM((RING, 32, 2 * CHUNK), BF),
-            pltpu.VMEM((RING, 32, 2 * CHUNK), BF),
+            pltpu.VMEM((2, RING, 32, CHUNK), BF),
+            pltpu.VMEM((2, RING, 32, CHUNK), BF),
             pltpu.VMEM((1024, 2 * NR), BF),
             pltpu.VMEM((1024, 2 * NR), BF),
-            pltpu.VMEM((2, 64, KPT, CHUNK), BF),
-            pltpu.VMEM((2, 64, KPT, CHUNK), BF),
-            pltpu.VMEM((2, 4, CHUNKS, KPT, CHUNK), BF),
+            pltpu.VMEM((2, 2, 64, KPT, 128), BF),
+            pltpu.VMEM((2, 2, 64, KPT, 128), BF),
+            pltpu.VMEM((2, 4, CHUNKS, 2, KPT, 128), BF),
             pltpu.VMEM((4, W * KPT, 128), F32),
             pltpu.VMEM((KPT, 256, 256), BF),
             pltpu.VMEM((KPT, W, 2 * W), BF),
             pltpu.VMEM((64, 1, 128), F32),
             pltpu.VMEM((8, 1, 128), F32),
-            dma, dma, dma, dma((2,)), dma((2,)), dma((2,)), dma((2,)), dma((2,)), dma, dma, dma((2,)), dma, dma((2,)), dma,
+            dma, dma, dma, dma((2,)), dma((2,)), dma((2,)), dma((2,)), dma((2,)), dma((2,)), dma, dma, dma((2,)), dma, dma((2,)), dma,
         ],
         compiler_params=pltpu.CompilerParams(
             collective_id=0, has_side_effects=True, vmem_limit_bytes=56 * 1024 * 1024
         ),
         name="orbital",
     )(kgrid, rvec, degen.reshape(1, NR), operators, vectors)
-    return density, magnet.reshape(3)
+    return result[0:3, 0:KPT], result[3, 0:3]
 
 
 def solution(mesh):

time: 54.1 us -> 53.2 us (0.983)
  Pallas kernels: 52.3 us -> 51.4 us
    unnamed x2 -> x0, local copies, waits for them, and re-layouts: 1.09 us -> none
    pallas_call x1, Pallas kernels: 52.3 us -> 51.4 us  [per_device(): pl.pallas_call(body, out_shape=pltpu.VMEM((8, 128), F32), in_specs=[anywh...]
    slice x0 -> x1, local copies, waits for them, and re-layouts: none -> 0.58 us  [per_device(): return (result[0:3, 0:KPT], result[3, 0:3])]
where the time goes in v6:
time: 53.2 us; the launch traced here: 53.1 us
  Pallas kernels  51.4 us (97%)
  local copies, waits for them, and re-layouts  1.09 us (2%)
  between operations  0.64 us (1%)
    pallas_call x1, Pallas kernels, per_device(): pl.pallas_call(body, out_shape=pltpu.VMEM((8, 128), F32), in_specs=[anywh...  51.4 us

profile of v6, /device:TPU:1, one launch (start us, length us, event | category | flops | bytes accessed | tf_op | source)
XLA Modules:
  0.0 53.1 jit_solution(10212003070706851961)
XLA Ops:
  0.6 51.4 %orbital.1 = f32[8,128]{1,0:T(8,128)S(1)} custom-call(s32[3,8]{1,0:T(4,128)} %kgrid_hbm.1, s32[3,256]{1,0:T(4,128)} %rvec_hbm.1, s32[1,256]{1,0:T(1,128)} %bitcast.3, bf16[1,2,12800]{2,1,0:T(2,128)(2,1)} %operators_hbm.1, bf16[8,12800]{1,0:T(8,128)(2,1)} %vectors.1), custom_call_target="tpu_custom_call" | custom-call | tf_op jit(solution)/shard_map/orbital/pallas_call | solution.py:489
  52.0 0.5 slice_bitcast_fusion
  52.5 0.6 %slice.6 = f32[3,8]{1,0:T(4,128)} slice(f32[8,128]{1,0:T(8,128)S(1)} %orbital.1), slice={[0:3], [0:8]} | slice | bytes 192 | tf_op jit(solution)/shard_map/slice | solution.py:525

commit v7 on v6

--- a/solution.py
+++ b/solution.py
@@ -361,7 +361,8 @@
 
             matrix_rows(lambda t: full[half, o, t // 2, t % 2].astype(F32), put)
 
-        each(4, rebuild)
+        for o in range(4):
+            rebuild(o)
         group = range(4)
         prods = []
         for k in group:
@@ -429,11 +430,8 @@
         for px, pc, _ in some:
             push(sums.at[xc * 8 + z], sums.at[xc * 8 + z], sum_send, sum_sem.at[0], at(px, y, pc, ring))
 
-    def tell_far(i):
-        half = lax.div(i + 1, 2)
-        tell(jnp.where(lax.rem(i, 2) == 0, 4 + half, 4 - half), columns)
-
-    each(7, tell_far)
+    for step in FAR:
+        tell(step, columns)
     tell(0, columns[:-1])
     eye = iota((KPT, 128), 0) == iota((KPT, 128), 1)
     for comp in range(3):

time: 53.2 us -> 53 us (level)
  no operation moved by 1% of the time
where the time goes in v7:
time: 53 us; the launch traced here: 52.8 us
  Pallas kernels  51.1 us (96%)
  local copies, waits for them, and re-layouts  1.09 us (2%)
  between operations  0.64 us (1%)
    pallas_call x1, Pallas kernels, per_device(): pl.pallas_call(body, out_shape=pltpu.VMEM((8, 128), F32), in_specs=[anywh...  51.1 us

profile of v7, /device:TPU:1, one launch (start us, length us, event | category | flops | bytes accessed | tf_op | source)
XLA Modules:
  0.0 52.8 jit_solution(11261394786180348294)
XLA Ops:
  0.6 51.1 %orbital.1 = f32[8,128]{1,0:T(8,128)S(1)} custom-call(s32[3,8]{1,0:T(4,128)} %kgrid_hbm.1, s32[3,256]{1,0:T(4,128)} %rvec_hbm.1, s32[1,256]{1,0:T(1,128)} %bitcast.3, bf16[1,2,12800]{2,1,0:T(2,128)(2,1)} %operators_hbm.1, bf16[8,12800]{1,0:T(8,128)(2,1)} %vectors.1), custom_call_target="tpu_custom_call" | custom-call | tf_op jit(solution)/shard_map/orbital/pallas_call | solution.py:487
  51.7 0.5 slice_bitcast_fusion
  52.3 0.6 %slice.6 = f32[3,8]{1,0:T(4,128)} slice(f32[8,128]{1,0:T(8,128)S(1)} %orbital.1), slice={[0:3], [0:8]} | slice | bytes 192 | tf_op jit(solution)/shard_map/slice | solution.py:523
